TPU v7x, 256 devices: a whole 4x4x8 slice. The times are simulated.
256 devices in a mesh: az: 64 (over x, z, core), rg: 4 (over y).
Axes of the slice: x: 4, y: 4, z: 8, core: 2. Of those that a mesh axis runs over, the one named last changes fastest.
Arguments:
- echoes: bfloat16 [2, 2048, 32768], P(None, 'rg', 'az'), may hold values from -6 to 6
- coef_table: bfloat16 [8, 5, 128, 128], replicated, may hold values from -0.3125 to 0.3125
- kern_id: int32 [256], replicated, may hold values from 0 to 7
- band_lo: int32 [256], replicated, may hold values from -2 to 2, as said below
- band_width: int32 [256], replicated, may hold values from 1 to 5
- rate: float32 [2048], P('rg'), may hold values from 4 to 40
Outputs:
- image: bfloat16 [2, 2048, 32768], P(None, ('rg', 'az'))
Inputs may be any that keep to these rules, and one draw needn't show every extreme that they name: band_lo[b] + band_width[b] - 1 <= 2 for every frequency block b.
All inputs are finite; a program needn't handle non-finite values.
Results may differ from a plain program's by a relative error of at most 0.0095.
Values may be sent and summed in bfloat16 or wider, within the bound.
No kernel may reach another device: no remote copies, remote signals or barrier semaphores. Data moves between devices by JAX's collectives and lax.ppermute only.
A program may use at most 64 MiB of HBM per device.

v0:
```python
import math

import jax
import jax.numpy as jnp
from jax import lax
from jax.sharding import PartitionSpec as P

A = 32768
P_SIZE = 512
Q = 64
TILE = 128
FB = 128
FBLK = 256
HT = 2
WMAX = 5


TWO_PI = 2.0 * math.pi


def padded_2(block, sides, width):
    for axis, dim in sides:
        count = lax.axis_size(axis)
        forward = [(i, i + 1) for i in range(count - 1)]
        backward = [(target, source) for source, target in forward]
        low = lax.ppermute(
            lax.slice_in_dim(block, block.shape[dim] - width, None, axis=dim), axis, forward
        )
        high = lax.ppermute(lax.slice_in_dim(block, 0, width, axis=dim), axis, backward)
        block = jnp.concatenate([low, block, high], axis=dim)
    return block


def rotation(first, second, length):
    product = lax.broadcasted_iota(jnp.int32, (first, second), 0) * lax.broadcasted_iota(
        jnp.int32, (first, second), 1
    )
    angle = (product % length).astype(jnp.float32) * (TWO_PI / length)
    return (jnp.cos(angle), jnp.sin(angle))


def tables():
    cosine_first, sine_first = rotation(P_SIZE, P_SIZE, P_SIZE)
    cosine_second, sine_second = rotation(Q, Q, Q)
    cosine_twist, sine_twist = rotation(Q, P_SIZE, A)
    scale_first = 1.0 / math.sqrt(P_SIZE)
    scale_second = 1.0 / math.sqrt(Q)
    return (
        (cosine_first * scale_first).astype(jnp.bfloat16),
        (sine_first * scale_first).astype(jnp.bfloat16),
        (cosine_second * scale_second).astype(jnp.bfloat16),
        (sine_second * scale_second).astype(jnp.bfloat16),
        cosine_twist,
        sine_twist,
    )


def contract(form, left, right):
    return jnp.einsum(form, left, right, preferred_element_type=jnp.float32)


def forward(planes, factors):
    cosine_first, sine_first, cosine_second, sine_second, cosine_twist, sine_twist = factors
    width = planes.shape[1]
    grid = planes.reshape(2, width, P_SIZE, Q)
    real_part = grid[0]
    imaginary = grid[1]
    first_real = contract("cpq,pf->cqf", real_part, cosine_first) + contract(
        "cpq,pf->cqf", imaginary, sine_first
    )
    first_imaginary = contract("cpq,pf->cqf", imaginary, cosine_first) - contract(
        "cpq,pf->cqf", real_part, sine_first
    )
    turned_real = (first_real * cosine_twist + first_imaginary * sine_twist).astype(jnp.bfloat16)
    turned_imaginary = (first_imaginary * cosine_twist - first_real * sine_twist).astype(
        jnp.bfloat16
    )
    second_real = contract("gq,cqf->cgf", cosine_second, turned_real) + contract(
        "gq,cqf->cgf", sine_second, turned_imaginary
    )
    second_imaginary = contract("gq,cqf->cgf", cosine_second, turned_imaginary) - contract(
        "gq,cqf->cgf", sine_second, turned_real
    )
    return jnp.stack([second_real, second_imaginary]).reshape(2, width, A).astype(jnp.bfloat16)


def inverse(planes, factors):
    cosine_first, sine_first, cosine_second, sine_second, cosine_twist, sine_twist = factors
    width = planes.shape[1]
    grid = planes.reshape(2, width, Q, P_SIZE)
    real_part = grid[0]
    imaginary = grid[1]
    first_real = contract("qg,cgf->cqf", cosine_second, real_part) - contract(
        "qg,cgf->cqf", sine_second, imaginary
    )
    first_imaginary = contract("qg,cgf->cqf", cosine_second, imaginary) + contract(
        "qg,cgf->cqf", sine_second, real_part
    )
    turned_real = (first_real * cosine_twist - first_imaginary * sine_twist).astype(jnp.bfloat16)
    turned_imaginary = (first_imaginary * cosine_twist + first_real * sine_twist).astype(
        jnp.bfloat16
    )
    second_real = contract("cqf,fp->cpq", turned_real, cosine_first) - contract(
        "cqf,fp->cpq", turned_imaginary, sine_first
    )
    second_imaginary = contract("cqf,fp->cpq", turned_imaginary, cosine_first) + contract(
        "cqf,fp->cpq", turned_real, sine_first
    )
    return jnp.stack([second_real, second_imaginary]).reshape(2, width, A).astype(jnp.bfloat16)


def body(echoes, coef_table, kern_id, band_lo, band_width, rate):
    factors = tables()
    members = lax.axis_size("az")
    here = lax.axis_index("az")
    range_rows = echoes.shape[1]
    lines = echoes.shape[2]
    columns = range_rows // members
    per_device = FBLK // members
    freq_dev = per_device * FB
    tiles = range_rows // TILE
    grouped = echoes.reshape(2, members, columns, lines)
    piece = lax.all_to_all(grouped, "az", split_axis=1, concat_axis=3, tiled=True)
    spectrum = forward(piece.reshape(2, piece.shape[2], A), factors)
    parted = spectrum.reshape(2, columns, members, freq_dev)
    turned = lax.all_to_all(parted, "az", split_axis=2, concat_axis=1, tiled=True)
    block_first = here * per_device
    block_stride = 1
    local = turned.reshape(2, range_rows, freq_dev)
    rim = HT * TILE
    padded = padded_2(local, (("rg", 1),), rim)

    def one_block(index, result):
        block = block_first + index * block_stride
        lower = band_lo[block]
        width = band_width[block]
        kernel = coef_table[kern_id[block]]
        columns_in = lax.dynamic_slice_in_dim(padded, index * FB, FB, 2)
        empty = jnp.zeros((2, tiles, TILE, FB), jnp.float32)
        total = empty
        for offset in range(WMAX):
            masked = jnp.where(offset < width, kernel[offset], jnp.zeros_like(kernel[offset]))
            start = (HT + lower + offset) * TILE
            slab = lax.dynamic_slice_in_dim(columns_in, start, range_rows, 1).reshape(
                2, tiles, TILE, FB
            )
            total = total + contract("ij,ptjf->ptif", masked, slab)
        moved = total.reshape(2, range_rows, FB)
        signed = (block * FB + lax.broadcasted_iota(jnp.int32, (FB,), 0) + A // 2) % A - A // 2
        doppler = signed.astype(jnp.float32) / A
        phase = rate[:, None] * (doppler * doppler)[None, :] * TWO_PI
        cosine = jnp.cos(phase)
        sine = jnp.sin(phase)
        focused_real = moved[0] * cosine + moved[1] * sine
        focused_imaginary = moved[1] * cosine - moved[0] * sine
        focused = jnp.stack([focused_real, focused_imaginary]).astype(jnp.bfloat16)
        return lax.dynamic_update_slice_in_dim(result, focused, index * FB, 2)

    filtered = lax.fori_loop(
        0, per_device, one_block, jnp.zeros((2, range_rows, freq_dev), jnp.bfloat16)
    )
    returned = filtered.reshape(2, members, columns, 1, freq_dev)
    piece = lax.all_to_all(returned, "az", split_axis=1, concat_axis=3, tiled=True)
    return inverse(piece.reshape(2, piece.shape[2], A), factors)


def solution(mesh):
    in_specs = (P(None, "rg", "az"), P(), P(), P(), P(), P("rg"))
    out_specs = P(None, ("rg", "az"), None)
    return jax.shard_map(body, mesh=mesh, in_specs=in_specs, out_specs=out_specs, check_vma=False)
```

profile of v0, /device:TPU:1, one launch (start us, length us, event | category | flops | bytes accessed | tf_op | source)
XLA Modules:
  0.0 264.5 jit_solution(644591594044299887)
XLA Ops:
  0.0 2.3 copy.28
  2.3 13.0 %all-to-all-start = ((bf16[2,64,8,512]{3,2,0,1:T(8,128)(2,1)}), bf16[2,64,8,512]{3,2,0,1:T(8,128)(2,1)S(1)}, u32[]{:S(2)}, u32[]{:S(2)}) async-start(bf16[2,64,8,512]{3,2,0,1:T(8,128)(2,1)} %copy.28), calls=%async_computation | async-start | bytes 2097152 | tf_op jit(solution)/shard_map/all_to_all | solution.py:123
  15.9 28.0 %all-to-all-done = bf16[2,64,8,512]{3,2,0,1:T(8,128)(2,1)S(1)} async-done(((bf16[2,64,8,512]{3,2,0,1:T(8,128)(2,1)}), bf16[2,64,8,512]{3,2,0,1:T(8,128)(2,1)S(1)}, u32[]{:S(2)}, u32[]{:S(2)}) %all-to-all-start) | async-done | bytes 1048608 | tf_op jit(solution)/shard_map/all_to_all | solution.py:123
  45.0 4.9 %fusion.71 = f32[512,512]{0,1:S(1)} fusion(bf16[512,512]{0,1:T(8,128)(2,1)S(1)} %bitcast.267), kind=kOutput, calls=%fused_computation.113 | convolution fusion | flops 272629760 | bytes 1572864
  49.9 5.7 %fusion.70 = f32[512,512]{0,1} fusion(bf16[512,512]{0,1:T(8,128)(2,1)S(1)} %bitcast.268), kind=kOutput, calls=%fused_computation.112 | convolution fusion | flops 272629760 | bytes 1572864
  56.6 4.9 %fusion.69 = f32[512,512]{0,1:S(1)} fusion(bf16[512,512]{0,1:T(8,128)(2,1)S(1)} %bitcast.269), kind=kOutput, calls=%fused_computation.111 | convolution fusion | flops 272629760 | bytes 1572864
  61.5 5.1 %fusion.72 = f32[512,512]{0,1:S(1)} fusion(bf16[512,512]{0,1:T(8,128)(2,1)S(1)} %bitcast.270), kind=kOutput, calls=%fused_computation.114 | convolution fusion | flops 272629760 | bytes 1572864
  69.5 34.5 %all_to_all.45 = bf16[2,8,64,512]{3,1,0,2:T(8,128)(2,1)S(1)} all-to-all(bf16[2,8,64,512]{3,1,0,2:T(8,128)(2,1)S(1)} %copy.35), channel_id=1, replica_groups=mesh['az'=64,'rg'=4] {'az'}, dimensions={2} | all-to-all | bytes 2097152 | tf_op jit(solution)/shard_map/all_to_all | solution.py:126
  104.2 3.2 %collective-permute-start = (bf16[2,256,512]{2,1,0:T(8,128)(2,1)S(1)}, bf16[2,256,512]{2,1,0:T(8,128)(2,1)S(1)}, u32[]{:S(2)}, u32[]{:S(2)}) collective-permute-start(bf16[2,256,512]{2,1,0:T(8,128)(2,1)S(1)} %get-tuple-element.310), channel_id=1, source_target_pairs={{0,1},{1,2},{2,3},{4,5},{5,6},{6,7},{8,9},{9,10},{10,11},{12,13},{... | collective-permute-start | bytes 1572872 | tf_op jit(solution)/shard_map/ppermute | solution.py:26
  107.5 1.3 collective-permute-start.1
  108.8 9.9 %collective-permute-done = bf16[2,256,512]{2,1,0:T(8,128)(2,1)S(1)} collective-permute-done((bf16[2,256,512]{2,1,0:T(8,128)(2,1)S(1)}, bf16[2,256,512]{2,1,0:T(8,128)(2,1)S(1)}, u32[]{:S(2)}, u32[]{:S(2)}) %collective-permute-start) | collective-permute-done | bytes 524320 | tf_op jit(solution)/shard_map/ppermute | solution.py:26
  119.5 3.1 %collective-permute-done.1 = bf16[2,256,512]{2,1,0:T(8,128)(2,1)} collective-permute-done((bf16[2,256,512]{2,1,0:T(8,128)(2,1)S(1)}, bf16[2,256,512]{2,1,0:T(8,128)(2,1)}, u32[]{:S(2)}, u32[]{:S(2)}) %collective-permute-start.1) | collective-permute-done | bytes 524320 | tf_op jit(solution)/shard_map/ppermute | solution.py:29
  122.6 1.3 pad_maximum_fusion
  125.0 75.2 %while.16 = (s32[]{:T(128)}, bf16[2,512,512]{2,1,0:T(8,128)(2,1)}, s32[]{:T(128)}, s32[256]{0:T(256)S(1)}, bf16[2,1024,512]{2,1,0:T(8,128)(2,1)S(1)}, /*index=5*...) while((s32[]{:T(128)}, bf16[2,512,512]{2,1,0:T(8,128)(2,1)}, ...), condition=%wide.region_1.2_spmd, body=%wide.region_0.1_spmd.sunk | while | flops 169560240 | bytes 11180494 | solution.py:159
  128.5 2.0 constant_dynamic-slice_fusion.6
  147.3 2.0 constant_dynamic-slice_fusion.6
  166.1 2.0 constant_dynamic-slice_fusion.6
  184.9 2.0 constant_dynamic-slice_fusion.6
  200.2 1.4 copy.37
  201.6 35.1 %all_to_all.46 = bf16[2,64,8,1,512]{4,2,0,3,1:T(8,128)(2,1)S(1)} all-to-all(bf16[2,64,8,1,512]{4,2,0,3,1:T(8,128)(2,1)S(1)} %copy.37), channel_id=1, replica_groups=mesh['az'=64,'rg'=4] {'az'}, dimensions={1} | all-to-all | bytes 2097152 | tf_op jit(solution)/shard_map/all_to_all | solution.py:163
  239.2 4.9 %fusion.67 = f32[512,8,64]{0,2,1:T(8,128)S(1)} fusion(bf16[8,64,512]{2,1,0:T(8,128)(2,1)S(1)} %get-tuple-element.308), kind=kOutput, calls=%fused_computation.109 | convolution fusion | flops 272629760 | bytes 1572864 | tf_op jit(solution)/shard_map/cqf,fp->cpq/dot_general | solution.py:59
  244.1 5.7 %fusion.65 = f32[512,8,64]{0,2,1:T(8,128)} fusion(bf16[8,64,512]{2,1,0:T(8,128)(2,1)S(1)} %get-tuple-element.309), kind=kOutput, calls=%fused_computation.107 | convolution fusion | flops 272629760 | bytes 1572864 | tf_op jit(solution)/shard_map/cqf,fp->cpq/dot_general | solution.py:59
  249.8 5.0 %fusion.50 = bf16[8,512,64]{1,2,0:T(8,128)(2,1)S(1)} fusion(f32[512,8,64]{0,2,1:T(8,128)S(1)} %fusion.67, bf16[8,64,512]{2,1,0:T(8,128)(2,1)S(1)} %get-tuple-element.309), kind=kOutput, calls=%fused_computation.78 | convolution fusion | flops 273154048 | bytes 2097152 | tf_op jit(solution)/shard_map/cqf,fp->cpq/dot_general | solution.py:59
  256.1 6.0 %fusion.49 = bf16[8,512,64]{1,2,0:T(8,128)(2,1)S(1)} fusion(f32[512,8,64]{0,2,1:T(8,128)} %fusion.65, bf16[8,64,512]{2,1,0:T(8,128)(2,1)S(1)} %get-tuple-element.308), kind=kOutput, calls=%fused_computation.77 | convolution fusion | flops 273154048 | bytes 2097152 | tf_op jit(solution)/shard_map/cqf,fp->cpq/dot_general | solution.py:59
  (92 shorter events, 50.8 us)
Async XLA Ops:
  2.3 41.5 %all-to-all-start = ((bf16[2,64,8,512]{3,2,0,1:T(8,128)(2,1)}), bf16[2,64,8,512]{3,2,0,1:T(8,128)(2,1)S(1)}, u32[]{:S(2)}, u32[]{:S(2)}) async-start(bf16[2,64,8,512]{3,2,0,1:T(8,128)(2,1)} %copy.28), calls=%async_computation | async-start | bytes 2097152 | tf_op jit(solution)/shard_map/all_to_all | solution.py:123
  15.9 50.7 %copy-start = (f32[64,512]{1,0:T(8,128)}, f32[64,512]{1,0:T(8,128)S(1)}, u32[]{:S(2)}) copy-start(f32[64,512]{1,0:T(8,128)S(1)} %get-tuple-element.315) | copy-start | bytes 393220
  61.5 5.1 %copy-start.2 = (f32[512,512]{0,1:S(1)}, f32[512,512]{0,1}, u32[]{:S(2)}) copy-start(f32[512,512]{0,1} %fusion.70) | copy-start | bytes 3145732
  104.2 14.5 %collective-permute-start = (bf16[2,256,512]{2,1,0:T(8,128)(2,1)S(1)}, bf16[2,256,512]{2,1,0:T(8,128)(2,1)S(1)}, u32[]{:S(2)}, u32[]{:S(2)}) collective-permute-start(bf16[2,256,512]{2,1,0:T(8,128)(2,1)S(1)} %get-tuple-element.310), channel_id=1, source_target_pairs={{0,1},{1,2},{2,3},{4,5},{5,6},{6,7},{8,9},{9,10},{10,11},{12,13},{... | collective-permute-start | bytes 1572872 | tf_op jit(solution)/shard_map/ppermute | solution.py:26
  107.5 15.2 %collective-permute-start.1 = (bf16[2,256,512]{2,1,0:T(8,128)(2,1)S(1)}, bf16[2,256,512]{2,1,0:T(8,128)(2,1)}, u32[]{:S(2)}, u32[]{:S(2)}) collective-permute-start(bf16[2,256,512]{2,1,0:T(8,128)(2,1)S(1)} %get-tuple-element.311), channel_id=1, source_target_pairs={{1,0},{2,1},{3,2},{5,4},{6,5},{7,6},{9,8},{10,9},{11,10},{13,12},{... | collective-permute-start | bytes 1572872 | tf_op jit(solution)/shard_map/ppermute | solution.py:29
  108.8 16.2 %copy-start.4 = (f32[512]{0:T(512)S(1)}, f32[512]{0:T(512)}, u32[]{:S(2)}) copy-start(f32[512]{0:T(512)} %param.13) | copy-start | bytes 6148
  108.8 16.2 %copy-start.5 = (s32[256]{0:T(256)S(1)}, s32[256]{0:T(256)}, u32[]{:S(2)}) copy-start(s32[256]{0:T(256)} %param.11) | copy-start | bytes 3076
  108.8 16.2 %copy-start.6 = (s32[256]{0:T(256)S(1)}, s32[256]{0:T(256)}, u32[]{:S(2)}) copy-start(s32[256]{0:T(256)} %param.12) | copy-start | bytes 3076
  108.8 16.2 %copy-start.7 = (s32[256]{0:T(256)S(1)}, s32[256]{0:T(256)}, u32[]{:S(2)}) copy-start(s32[256]{0:T(256)} %param.10) | copy-start | bytes 3076
  118.7 0.8 copy-start.3
  237.7 0.9 copy-start.1
where the time goes:
time: 266 us; the launch traced here: 264 us
  blocking collectives  69.7 us (26%)
  matrix products  67.5 us (25%)
  waiting for transfers between devices  41 us (15%)
  loops' own time  29.9 us (11%)
  local copies, waits for them, and re-layouts  26.9 us (10%)
  starting transfers between devices  17.5 us (7%)
  other arithmetic  11.6 us (4%)
    dot_general x32, matrix products, contract(): return jnp.einsum(form, left, right, preferred_element_type=jnp.float32)  47 us
    all_to_all x1, blocking collectives, body(): lax.all_to_all(returned, 'az', split_axis=1, concat_axis=3, tiled=True)  35.1 us
    all_to_all x1, blocking collectives, body(): lax.all_to_all(parted, 'az', split_axis=2, concat_axis=1, tiled=True)  34.5 us
    another operation x1, loops' own time, body(): lax.fori_loop(0, per_device, one_block, jnp.zeros((2, range_rows, freq_de...  29.9 us
    all_to_all x1, waiting for transfers between devices, body(): lax.all_to_all(grouped, 'az', split_axis=1, concat_axis=3, tiled=True)  28 us
    unnamed x4, matrix products  20.5 us
    all_to_all x1, starting transfers between devices, body(): lax.all_to_all(grouped, 'az', split_axis=1, concat_axis=3, tiled=True)  13 us
    ppermute x1, waiting for transfers between devices, padded_2(): lax.ppermute(lax.slice_in_dim(block, block.shape[dim] - width, None, axis...  9.87 us
  transfers between devices with their start and end apart: 3, of which 3 were waited for; matrix products, arithmetic and copies ran while one was open for 0% of the time, Pallas kernels for 0%

commit v1 on v0

v1 whole, which is shorter than its diff:
```python
import functools
import math

import jax
import jax.numpy as jnp
import ml_dtypes
import numpy as np
from jax import lax
from jax.experimental import pallas as pl
from jax.experimental.pallas import tpu as pltpu
from jax.sharding import PartitionSpec as P

A = 32768
P_SIZE = 512
Q = 64
R = 2048
TILE = 128
FB = 128
FBLK = 256
HT = 2
WMAX = 5
ROWS = 8
HALF = 64
LIMIT = 48 * 1024 * 1024


def angles(first, second, length):
    product = np.outer(np.arange(first), np.arange(second)) % length
    turn = product * (2.0 * math.pi / length)
    return np.cos(turn), np.sin(turn)


def rounded(values):
    return values.astype(np.float32).astype(ml_dtypes.bfloat16)


@functools.lru_cache(maxsize=None)
def tables():
    cosine, sine = angles(P_SIZE, P_SIZE, P_SIZE)
    cosine, sine = cosine / math.sqrt(P_SIZE), sine / math.sqrt(P_SIZE)
    whole = np.zeros((2, P_SIZE, 2, P_SIZE))
    whole[0, :, 0] = cosine
    whole[0, :, 1] = sine
    whole[1, :, 1] = cosine
    whole[1, :, 0] = -sine
    first = whole.reshape(2, 4, 128, 2, 64, 4, 2).transpose(1, 0, 2, 4, 6, 3, 5).reshape(1024, 1024)
    back = np.zeros((2, P_SIZE, 2, P_SIZE))
    back[0, :, 0] = cosine
    back[0, :, 1] = -sine
    back[1, :, 1] = cosine
    back[1, :, 0] = sine
    last = back.reshape(2, 2, 128, 2, 2, P_SIZE).transpose(0, 1, 3, 2, 4, 5).reshape(1024, 1024)
    cosine, sine = angles(Q, Q, Q)
    cosine, sine = cosine / math.sqrt(Q), sine / math.sqrt(Q)
    eye = np.eye(ROWS)
    small = np.zeros((2, Q, 2, Q))
    small[0, :, 0] = cosine
    small[0, :, 1] = sine
    small[1, :, 1] = cosine
    small[1, :, 0] = -sine
    second = np.einsum("pgqa,rs->gprqsa", small, eye).reshape(1024, 1024)
    small = np.zeros((2, Q, 2, Q))
    small[0, :, 0] = cosine
    small[0, :, 1] = -sine
    small[1, :, 1] = cosine
    small[1, :, 0] = sine
    third = np.einsum("paqg,rs->rpagqs", small, eye)
    third = third.reshape(4, 2, 2, Q, Q, 2, ROWS).transpose(0, 2, 1, 3, 4, 5, 6).reshape(1024, 1024)
    cosine, sine = angles(Q, P_SIZE, A)
    turned = [np.tile(part.T, (1, 2)).astype(np.float32) for part in (cosine, sine)]
    straight = [np.tile(part, (2, 1)).astype(np.float32) for part in (cosine, sine)]
    return (rounded(first), rounded(second), *turned), (rounded(third), rounded(last), *straight)


def pack_kernel(echo_ref, out_ref, stage):
    low = lax.broadcasted_iota(jnp.int32, (8, 128), 1) < HALF
    for dest in range(echo_ref.shape[1] // ROWS):
        for plane in range(2):
            rows = echo_ref[plane, dest * ROWS : (dest + 1) * ROWS, :].astype(jnp.float32)
            for part in range(4):
                stage[pl.ds((dest * 8 + plane * 4 + part) * 8, 8), :] = rows[:, part * 128 : (part + 1) * 128]
    for dest in range(echo_ref.shape[1] // ROWS):
        for pair in range(4):
            even = stage[pl.ds(dest * 64 + 2 * pair, 8, stride=8), :]
            odd = stage[pl.ds(dest * 64 + 2 * pair + 1, 8, stride=8), :]
            lower = jnp.where(low, even, pltpu.roll(odd, HALF, 1))
            upper = jnp.where(low, pltpu.roll(even, HALF, 1), odd)
            both = jnp.concatenate([lower, upper], axis=0).astype(jnp.bfloat16)
            out_ref[dest, :, pair * 128 : (pair + 1) * 128] = both


def pack(echoes):
    steps = 4
    rows = 512 // steps
    return pl.pallas_call(
        pack_kernel,
        grid=(steps,),
        in_specs=[pl.BlockSpec((2, rows, 512), lambda i: (0, i, 0))],
        out_specs=pl.BlockSpec((rows // ROWS, 16, 512), lambda i: (i, 0, 0)),
        out_shape=jax.ShapeDtypeStruct((64, 16, 512), jnp.bfloat16),
        scratch_shapes=[pltpu.VMEM((rows * 8, 128), jnp.float32)],
        compiler_params=pltpu.CompilerParams(vmem_limit_bytes=LIMIT),
        name="pack",
    )(echoes)


def forward_kernel(x_ref, first_ref, second_ref, cos_ref, sin_ref, out_ref, turned):
    for chunk in range(4):
        sums = jnp.dot(
            first_ref[chunk * 256 : (chunk + 1) * 256, :], x_ref[...], preferred_element_type=jnp.float32
        )
        cosine = cos_ref[chunk * 128 : (chunk + 1) * 128, :]
        sine = sin_ref[chunk * 128 : (chunk + 1) * 128, :]
        for pair in range(4):
            real = sums[:128, pair * 128 : (pair + 1) * 128]
            imaginary = sums[128:, pair * 128 : (pair + 1) * 128]
            span = slice(chunk * 128, (chunk + 1) * 128)
            turned[span, pair * 128 : (pair + 1) * 128] = (real * cosine + imaginary * sine).astype(jnp.bfloat16)
            turned[span, 512 + pair * 128 : 512 + (pair + 1) * 128] = (
                imaginary * cosine - real * sine
            ).astype(jnp.bfloat16)
    for chunk in range(4):
        sums = lax.dot_general(
            second_ref[chunk * 256 : (chunk + 1) * 256, :],
            turned[...],
            (((1,), (1,)), ((), ())),
            preferred_element_type=jnp.float32,
        ).astype(jnp.bfloat16)
        for part in range(4):
            out_ref[chunk * 16 : (chunk + 1) * 16, part] = sums[:, part * 128 : (part + 1) * 128].reshape(16, 16, 128)


def forward(x, first, second, cosine, sine):
    return pl.pallas_call(
        forward_kernel,
        out_shape=jax.ShapeDtypeStruct((64, 4, 16, 128), jnp.bfloat16),
        in_specs=[pl.BlockSpec(memory_space=pltpu.VMEM)] * 5,
        out_specs=pl.BlockSpec(memory_space=pltpu.VMEM),
        scratch_shapes=[pltpu.VMEM((512, 1024), jnp.bfloat16)],
        compiler_params=pltpu.CompilerParams(vmem_limit_bytes=LIMIT),
        name="forward",
    )(x, first, second, cosine, sine)


def migrate_kernel(band_ref, spectrum_ref, coef_ref, out_ref, taps, padded):
    lower = band_ref[1]
    width = band_ref[2]
    empty = jnp.zeros((TILE, TILE), jnp.bfloat16)
    taps[:TILE, 5 * TILE :] = empty
    taps[TILE:, :TILE] = empty
    for shift in range(WMAX):
        index = shift - HT - lower
        held = jnp.logical_and(index >= 0, index < width)
        weight = coef_ref[0, jnp.clip(index, 0, WMAX - 1)]
        scale = jnp.where(held, jnp.float32(1), jnp.float32(0))
        weight = (weight.astype(jnp.float32) * scale).astype(jnp.bfloat16)
        taps[:TILE, shift * TILE : (shift + 1) * TILE] = weight
        taps[TILE:, (shift + 1) * TILE : (shift + 2) * TILE] = weight
    rim = jnp.zeros((HT * TILE, 2 * FB), jnp.bfloat16)
    padded[: HT * TILE, :] = rim
    padded[HT * TILE + R :, :] = rim
    for block in range(8):
        values = spectrum_ref[block * 32 : (block + 1) * 32].astype(jnp.float32)
        start = HT * TILE + block * 256
        for plane in range(2):
            rows = values[:, plane * ROWS : (plane + 1) * ROWS, :].reshape(256, FB)
            padded[start : start + 256, plane * FB : (plane + 1) * FB] = rows.astype(jnp.bfloat16)
    for block in range(8):
        moved = jnp.dot(
            taps[...], padded[block * 256 : block * 256 + 6 * TILE, :], preferred_element_type=jnp.float32
        )
        real = moved[:, :FB].reshape(32, ROWS, FB)
        imaginary = moved[:, FB:].reshape(32, ROWS, FB)
        out_ref[block * 32 : (block + 1) * 32] = jnp.concatenate([real, imaginary], axis=1).astype(jnp.bfloat16)


def migrate(band, spectrum, coef_table):
    return pl.pallas_call(
        migrate_kernel,
        grid_spec=pltpu.PrefetchScalarGridSpec(
            num_scalar_prefetch=1,
            grid=(1,),
            in_specs=[
                pl.BlockSpec((256, 16, 128), lambda i, band: (0, 0, 0)),
                pl.BlockSpec((1, WMAX, TILE, TILE), lambda i, band: (band[0], 0, 0, 0)),
            ],
            out_specs=pl.BlockSpec((256, 16, 128), lambda i, band: (0, 0, 0)),
            scratch_shapes=[
                pltpu.VMEM((256, 6 * TILE), jnp.bfloat16),
                pltpu.VMEM((R + 2 * HT * TILE, 2 * FB), jnp.bfloat16),
            ],
        ),
        out_shape=jax.ShapeDtypeStruct((256, 16, 128), jnp.bfloat16),
        compiler_params=pltpu.CompilerParams(vmem_limit_bytes=LIMIT),
        name="migrate",
    )(band, spectrum, coef_table)


def rotor(turns):
    quarter = jnp.round(turns * 4.0)
    x = (turns - quarter * 0.25) * (2.0 * math.pi)
    square = x * x
    sine = x + x * square * (-1.0 / 6 + square * (1.0 / 120 + square * (-1.0 / 5040)))
    cosine = 1.0 + square * (-0.5 + square * (1.0 / 24 + square * (-1.0 / 720 + square * (1.0 / 40320))))
    count = quarter.astype(jnp.int32)
    swapped = (count & 1) == 1
    first = jnp.where(swapped, sine, cosine)
    second = jnp.where(swapped, cosine, sine)
    first = jnp.where(((count + 1) & 2) == 2, -first, first)
    second = jnp.where((count & 2) == 2, -second, second)
    return first, second


def inverse_kernel(moved_ref, rate_ref, third_ref, last_ref, cos_ref, sin_ref, out_ref, focused, turned, stage):
    rate = rate_ref[...]
    lane = lax.broadcasted_iota(jnp.int32, (16, ROWS, FB), 2)
    step = lax.broadcasted_iota(jnp.int32, (16, ROWS, FB), 0)
    for chunk in range(4):
        for part in range(4):
            frequency = (step + chunk * 16) * P_SIZE + (lane + part * FB)
            signed = jnp.where(frequency >= A // 2, frequency - A, frequency).astype(jnp.float32)
            doppler = signed * (1.0 / A)
            cosine, sine = rotor(rate[None] * (doppler * doppler))
            values = moved_ref[chunk * 16 : (chunk + 1) * 16, part].astype(jnp.float32)
            real, imaginary = values[:, :ROWS, :], values[:, ROWS:, :]
            both = jnp.concatenate(
                [real * cosine + imaginary * sine, imaginary * cosine - real * sine], axis=1
            ).astype(jnp.bfloat16)
            focused[chunk * 256 : (chunk + 1) * 256, part * FB : (part + 1) * FB] = both.reshape(256, FB)
    for chunk in range(4):
        sums = jnp.dot(
            third_ref[chunk * 256 : (chunk + 1) * 256, :], focused[...], preferred_element_type=jnp.float32
        )
        real, imaginary = sums[:128], sums[128:]
        cosine, sine = cos_ref[...], sin_ref[...]
        span = slice(chunk * 128, (chunk + 1) * 128)
        turned[span, :512] = (real * cosine - imaginary * sine).astype(jnp.bfloat16)
        turned[span, 512:] = (imaginary * cosine + real * sine).astype(jnp.bfloat16)
    low = lax.broadcasted_iota(jnp.int32, (128, 128), 1) < HALF
    for chunk in range(4):
        sums = lax.dot_general(
            last_ref[chunk * 256 : (chunk + 1) * 256, :],
            turned[...],
            (((1,), (1,)), ((), ())),
            preferred_element_type=jnp.float32,
        )
        for pair in range(4):
            even = sums[:128, pair * 128 : (pair + 1) * 128]
            odd = sums[128:, pair * 128 : (pair + 1) * 128]
            stage[pl.ds(2 * pair, 128, stride=8), :] = jnp.where(low, even, pltpu.roll(odd, HALF, 1))
            stage[pl.ds(2 * pair + 1, 128, stride=8), :] = jnp.where(low, pltpu.roll(even, HALF, 1), odd)
        plane, base = chunk // 2, (chunk % 2) * 128
        for group in range(128):
            out_ref[plane, :, (base + group) * 128 : (base + group + 1) * 128] = stage[
                group * 8 : (group + 1) * 8, :
            ].astype(jnp.bfloat16)


def inverse(moved, rate, third, last, cosine, sine):
    return pl.pallas_call(
        inverse_kernel,
        out_shape=jax.ShapeDtypeStruct((2, ROWS, A), jnp.bfloat16),
        in_specs=[pl.BlockSpec(memory_space=pltpu.VMEM)] * 6,
        out_specs=pl.BlockSpec(memory_space=pltpu.VMEM),
        scratch_shapes=[
            pltpu.VMEM((1024, 512), jnp.bfloat16),
            pltpu.VMEM((512, 1024), jnp.bfloat16),
            pltpu.VMEM((1024, 128), jnp.float32),
        ],
        compiler_params=pltpu.CompilerParams(vmem_limit_bytes=LIMIT),
        name="inverse",
    )(moved, rate, third, last, cosine, sine)


def body(echoes, coef_table, kern_id, band_lo, band_width, rate):
    ahead, behind = tables()
    az = lax.axis_index("az")
    block = lax.axis_index("rg") * lax.axis_size("az") + az
    band = jnp.stack([kern_id[block], band_lo[block], band_width[block]])
    rates = jnp.broadcast_to(lax.dynamic_slice(rate, (az * ROWS,), (ROWS,))[:, None], (ROWS, FB))
    piece = lax.all_to_all(pack(echoes), "az", 0, 0, tiled=True)
    spectrum = forward(piece.reshape(1024, 512), *ahead)
    spectrum = lax.all_to_all(spectrum.reshape(256, 16, 128), ("rg", "az"), 0, 0, tiled=True)
    moved = migrate(band, spectrum, coef_table)
    moved = lax.all_to_all(moved, ("rg", "az"), 0, 0, tiled=True)
    return inverse(moved.reshape(64, 4, 16, 128), rates, *behind)


def solution(mesh):
    in_specs = (P(None, "rg", "az"), P(), P(), P(), P(), P("rg"))
    out_specs = P(None, ("rg", "az"), None)
    return jax.shard_map(body, mesh=mesh, in_specs=in_specs, out_specs=out_specs, check_vma=False)
```

time: 266 us -> 140 us (0.53)
  matrix products: 67.5 us -> 0 us
  loops' own time: 29.9 us -> 0 us
  blocking collectives: 69.7 us -> 41.3 us
  local copies, waits for them, and re-layouts: 26.9 us -> 7.9 us
  waiting for transfers between devices: 41 us -> 59.8 us
  Pallas kernels: 0 us -> 14.1 us
  other arithmetic: 11.6 us -> 1.87 us
  starting transfers between devices: 17.5 us -> 14 us
    dot_general x32 -> x0, matrix products: 47 us -> none  [contract(): return jnp.einsum(form, left, right, preferred_element_type=jnp.float32)]
    all_to_all x1 -> x2, waiting for transfers between devices: 28 us -> 59.8 us  [the longest x1 31 us: body(): moved = lax.all_to_all(moved, ('rg', 'az'), 0, 0, tiled=True)]
    another operation x1 -> x0, loops' own time: 29.9 us -> none  [body(): lax.fori_loop(0, per_device, one_block, jnp.zeros((2, range_rows, freq_de...]
    all_to_all x2 -> x1, blocking collectives: 69.7 us -> 41.3 us  [body(): piece = lax.all_to_all(pack(echoes), 'az', 0, 0, tiled=True)]
    unnamed x4 -> x0, matrix products: 20.5 us -> none
    pallas_call x0 -> x4, Pallas kernels: none -> 14.1 us  [the longest x1 5.55 us: inverse(): pl.pallas_call(inverse_kernel, out_shape=jax.ShapeDtypeStruct((2, ROWS, A...]
    ppermute x2 -> x0, waiting for transfers between devices: 13 us -> none  [the longest x1 9.87 us: padded_2(): lax.ppermute(lax.slice_in_dim(block, block.shape[dim] - width, None, axis...]
    dynamic_slice x16 -> x4, local copies, waits for them, and re-layouts: 15 us -> 2.57 us  [the longest x3 1.81 us: body(): band = jnp.stack([kern_id[block], band_lo[block], band_width[block]])]
  transfers between devices with their start and end apart: 3 -> 2, of which waited for: 3 -> 2; matrix products, arithmetic and copies ran while one was open for 0% -> 3% of each run, Pallas kernels for 0% -> 0%
where the time goes in v1:
time: 140 us; the launch traced here: 139 us
  waiting for transfers between devices  59.8 us (43%)
  blocking collectives  41.3 us (30%)
  Pallas kernels  14.1 us (10%)
  starting transfers between devices  14 us (10%)
  local copies, waits for them, and re-layouts  7.9 us (6%)
  other arithmetic  1.87 us (1%)
    all_to_all x1, blocking collectives, body(): piece = lax.all_to_all(pack(echoes), 'az', 0, 0, tiled=True)  41.3 us
    all_to_all x1, waiting for transfers between devices, body(): moved = lax.all_to_all(moved, ('rg', 'az'), 0, 0, tiled=True)  31 us
    all_to_all x1, waiting for transfers between devices, body(): lax.all_to_all(spectrum.reshape(256, 16, 128), ('rg', 'az'), 0, 0, tiled=...  28.7 us
    all_to_all x1, starting transfers between devices, body(): lax.all_to_all(spectrum.reshape(256, 16, 128), ('rg', 'az'), 0, 0, tiled=...  8.87 us
    pallas_call x1, Pallas kernels, inverse(): pl.pallas_call(inverse_kernel, out_shape=jax.ShapeDtypeStruct((2, ROWS, A...  5.55 us
    unnamed x24, local copies, waits for them, and re-layouts  5.26 us
    all_to_all x1, starting transfers between devices, body(): moved = lax.all_to_all(moved, ('rg', 'az'), 0, 0, tiled=True)  5.18 us
    pallas_call x1, Pallas kernels, forward(): pl.pallas_call(forward_kernel, out_shape=jax.ShapeDtypeStruct((64, 4, 16,...  5.13 us
  transfers between devices with their start and end apart: 2, of which 2 were waited for; matrix products, arithmetic and copies ran while one was open for 3% of the time, Pallas kernels for 0%

profile of v1, /device:TPU:1, one launch (start us, length us, event | category | flops | bytes accessed | tf_op | source)
XLA Modules:
  0.0 139.1 jit_solution(8839130670527783542)
XLA Ops:
  0.0 1.4 copy-done.4
  1.4 0.9 pack.1
  2.3 41.3 %all_to_all.15 = bf16[64,16,512]{2,1,0:T(8,128)(2,1)S(1)} all-to-all(bf16[64,16,512]{2,1,0:T(8,128)(2,1)S(1)} %pack.1), channel_id=1, replica_groups=mesh['az'=64,'rg'=4] {'az'}, dimensions={0} | all-to-all | bytes 2097152 | tf_op jit(solution)/shard_map/all_to_all | solution.py:281
  43.6 0.0 copy-done.2
  43.6 0.0 copy-done.7
  43.6 0.0 copy-done.8
  43.6 5.1 %forward.1 = bf16[64,4,16,128]{3,2,1,0:T(8,128)(2,1)} custom-call(bf16[1024,512]{1,0:T(8,128)(2,1)S(1)} %bitcast.4, bf16[1024,1024]{1,0:T(8,128)(2,1)S(1)} %copy-done.2, bf16[1024,1024]{1,0:T(8,128)(2,1)} %constant.36.clone.second_ref, f32[512,128]{1,0:T(8,128)S(1)} %copy-done.7, f32[512,128]{1,0:T(8,128)S(1)} %copy-done.8), custom_call_target="tpu_custom_call" | custom-call | tf_op jit(solution)/shard_map/forward/pallas_call | solution.py:134
  48.8 8.9 %all-to-all-start.1 = ((bf16[256,16,128]{2,1,0:T(8,128)(2,1)}), bf16[256,16,128]{2,1,0:T(8,128)(2,1)S(1)}, u32[]{:S(2)}, u32[]{:S(2)}) async-start(bf16[256,16,128]{2,1,0:T(8,128)(2,1)} %bitcast.1), calls=%async_computation.1 | async-start | bytes 2097152 | tf_op jit(solution)/shard_map/all_to_all | solution.py:283
  57.7 0.6 dynamic_slice.12
  58.2 0.0 copy-done.10
  58.2 0.6 dynamic_slice.13
  58.8 0.6 dynamic_slice.14
  59.5 1.9 %pad_add_fusion.band_ref = s32[3]{0:T(128)S(1)} fusion(s32[1]{0:T(128)} %dynamic_slice.14, s32[1]{0:T(128)} %dynamic_slice.13, s32[1]{0:T(128)} %dynamic_slice.12), kind=kLoop, calls=%fused_computation | loop fusion | flops 6 | bytes 24 | tf_op jit(solution)/shard_map/stack | solution.py:279
  61.3 28.7 %all-to-all-done.1.spectrum_ref = bf16[256,16,128]{2,1,0:T(8,128)(2,1)S(1)} async-done(((bf16[256,16,128]{2,1,0:T(8,128)(2,1)}), bf16[256,16,128]{2,1,0:T(8,128)(2,1)S(1)}, u32[]{:S(2)}, u32[]{:S(2)}) %all-to-all-start.1) | async-done | bytes 1048608 | tf_op jit(solution)/shard_map/all_to_all | solution.py:283
  90.1 1.3 copy-done.3
  91.4 2.5 %migrate.1 = bf16[256,16,128]{2,1,0:T(8,128)(2,1)} custom-call(s32[3]{0:T(128)S(1)} %pad_add_fusion.band_ref, bf16[256,16,128]{2,1,0:T(8,128)(2,1)S(1)} %all-to-all-done.1.spectrum_ref, bf16[8,5,128,128]{3,2,1,0:T(8,128)(2,1)S(1)} %copy-done.3), custom_call_target="tpu_custom_call" | custom-call | tf_op jit(solution)/shard_map/migrate/pallas_call | solution.py:178
  94.0 5.2 %all-to-all-start.2 = ((bf16[256,16,128]{2,1,0:T(8,128)(2,1)}), bf16[256,16,128]{2,1,0:T(8,128)(2,1)S(1)}, u32[]{:S(2)}, u32[]{:S(2)}) async-start(bf16[256,16,128]{2,1,0:T(8,128)(2,1)} %migrate.1), calls=%async_computation.2 | async-start | bytes 2097152 | tf_op jit(solution)/shard_map/all_to_all | solution.py:285
  99.1 0.8 dynamic_slice.15
  99.9 31.0 %all-to-all-done.2 = bf16[256,16,128]{2,1,0:T(8,128)(2,1)S(1)} async-done(((bf16[256,16,128]{2,1,0:T(8,128)(2,1)}), bf16[256,16,128]{2,1,0:T(8,128)(2,1)S(1)}, u32[]{:S(2)}, u32[]{:S(2)}) %all-to-all-start.2) | async-done | bytes 1048608 | tf_op jit(solution)/shard_map/all_to_all | solution.py:285
  131.0 0.1 broadcast_in_dim.2.rate_ref
  131.0 0.0 copy-done.5
  131.0 1.6 %copy-done.1 = bf16[1024,1024]{1,0:T(8,128)(2,1)S(1)} copy-done((bf16[1024,1024]{1,0:T(8,128)(2,1)S(1)}, bf16[1024,1024]{1,0:T(8,128)(2,1)}, u32[]{:S(2)}) %copy-start.1) | copy-done | bytes 2097176
  132.6 0.9 copy-done.6
  133.6 5.5 %inverse.1 = bf16[2,8,32768]{2,1,0:T(8,128)(2,1)} custom-call(bf16[64,4,16,128]{3,2,1,0:T(8,128)(2,1)S(1)} %bitcast.3, f32[8,128]{1,0:T(8,128)S(1)} %broadcast_in_dim.2.rate_ref, bf16[1024,1024]{1,0:T(8,128)(2,1)S(1)} %copy-done, bf16[1024,1024]{1,0:T(8,128)(2,1)S(1)} %copy-done.1, f32[128,512]{1,0:T(8,128)S(1)} %copy-done.5, f32[128,512]{1,0:T(8,128)S(1)} %copy-done.6), custom_call_target="tpu_custom_call" | custom-call | tf_op jit(solution)/shard_map/inverse/pallas_call | solution.py:260
  (15 shorter events, 0.0 us)
Async XLA Ops:
  0.0 43.6 %copy-start.2 = (bf16[1024,1024]{1,0:T(8,128)(2,1)S(1)}, bf16[1024,1024]{1,0:T(8,128)(2,1)}, u32[]{:S(2)}) copy-start(bf16[1024,1024]{1,0:T(8,128)(2,1)} %constant.35.clone.first_ref) | copy-start | bytes 6291460
  0.0 1.4 copy-start.4
  1.4 42.2 %copy-start.7 = (f32[512,128]{1,0:T(8,128)S(1)}, f32[512,128]{1,0:T(8,128)}, u32[]{:S(2)}) copy-start(f32[512,128]{1,0:T(8,128)} %constant.37.clone.cos_ref) | copy-start | bytes 786436
  1.4 42.2 %copy-start.8 = (f32[512,128]{1,0:T(8,128)S(1)}, f32[512,128]{1,0:T(8,128)}, u32[]{:S(2)}) copy-start(f32[512,128]{1,0:T(8,128)} %constant.38.clone.sin_ref) | copy-start | bytes 786436
  48.8 8.9 %copy-start.9 = (s32[256]{0:T(256)S(1)}, s32[256]{0:T(256)}, u32[]{:S(2)}) copy-start(s32[256]{0:T(256)} %param.16) | copy-start | bytes 3076
  48.8 9.5 %copy-start.10 = (s32[256]{0:T(256)S(1)}, s32[256]{0:T(256)}, u32[]{:S(2)}) copy-start(s32[256]{0:T(256)} %param.17) | copy-start | bytes 3076
  48.8 10.1 %copy-start.11 = (s32[256]{0:T(256)S(1)}, s32[256]{0:T(256)}, u32[]{:S(2)}) copy-start(s32[256]{0:T(256)} %param.18) | copy-start | bytes 3076
  48.8 41.3 %all-to-all-start.1 = ((bf16[256,16,128]{2,1,0:T(8,128)(2,1)}), bf16[256,16,128]{2,1,0:T(8,128)(2,1)S(1)}, u32[]{:S(2)}, u32[]{:S(2)}) async-start(bf16[256,16,128]{2,1,0:T(8,128)(2,1)} %bitcast.1), calls=%async_computation.1 | async-start | bytes 2097152 | tf_op jit(solution)/shard_map/all_to_all | solution.py:283
  61.3 69.7 %copy-start = (bf16[1024,1024]{1,0:T(8,128)(2,1)S(1)}, bf16[1024,1024]{1,0:T(8,128)(2,1)}, u32[]{:S(2)}) copy-start(bf16[1024,1024]{1,0:T(8,128)(2,1)} %constant.39.clone.third_ref) | copy-start | bytes 6291460
  90.1 1.3 copy-start.3
  91.4 39.6 %copy-start.5 = (f32[128,512]{1,0:T(8,128)S(1)}, f32[128,512]{1,0:T(8,128)}, u32[]{:S(2)}) copy-start(f32[128,512]{1,0:T(8,128)} %constant.41.clone.cos_ref) | copy-start | bytes 786436
  94.0 37.0 %all-to-all-start.2 = ((bf16[256,16,128]{2,1,0:T(8,128)(2,1)}), bf16[256,16,128]{2,1,0:T(8,128)(2,1)S(1)}, u32[]{:S(2)}, u32[]{:S(2)}) async-start(bf16[256,16,128]{2,1,0:T(8,128)(2,1)} %migrate.1), calls=%async_computation.2 | async-start | bytes 2097152 | tf_op jit(solution)/shard_map/all_to_all | solution.py:285
  131.0 1.6 %copy-start.1 = (bf16[1024,1024]{1,0:T(8,128)(2,1)S(1)}, bf16[1024,1024]{1,0:T(8,128)(2,1)}, u32[]{:S(2)}) copy-start(bf16[1024,1024]{1,0:T(8,128)(2,1)} %constant.40.clone.last_ref) | copy-start | bytes 6291460
  132.6 0.9 copy-start.6

commit v2 on v1

v2 whole, which is shorter than its diff:
```python
import functools
import math

import jax
import jax.numpy as jnp
import ml_dtypes
import numpy as np
from jax import lax
from jax.experimental import pallas as pl
from jax.experimental.pallas import tpu as pltpu
from jax.sharding import PartitionSpec as P

A = 32768
P_SIZE = 512
Q = 64
R = 2048
TILE = 128
FB = 128
FBLK = 256
HT = 2
WMAX = 5
ROWS = 8
PACKS = 8
HALF = 64
MIB = 1024 * 1024
FAR = pltpu.MemorySpace.HBM
NEAR = pltpu.MemorySpace.VMEM


def angles(first, second, length):
    product = np.outer(np.arange(first), np.arange(second)) % length
    turn = product * (2.0 * math.pi / length)
    return np.cos(turn), np.sin(turn)


def rounded(values):
    return values.astype(np.float32).astype(ml_dtypes.bfloat16)


@functools.lru_cache(maxsize=None)
def tables():
    cosine, sine = angles(P_SIZE, P_SIZE, P_SIZE)
    cosine, sine = cosine / math.sqrt(P_SIZE), sine / math.sqrt(P_SIZE)
    whole = np.zeros((2, P_SIZE, 2, P_SIZE))
    whole[0, :, 0] = cosine
    whole[0, :, 1] = sine
    whole[1, :, 1] = cosine
    whole[1, :, 0] = -sine
    first = whole.reshape(2, 4, 128, 2, 64, 4, 2).transpose(1, 0, 2, 4, 6, 3, 5).reshape(1024, 1024)
    back = np.zeros((2, P_SIZE, 2, P_SIZE))
    back[0, :, 0] = cosine
    back[0, :, 1] = -sine
    back[1, :, 1] = cosine
    back[1, :, 0] = sine
    last = back.reshape(2, 2, 128, 2, 2, P_SIZE).transpose(0, 1, 3, 2, 4, 5).reshape(1024, 1024)
    cosine, sine = angles(Q, Q, Q)
    cosine, sine = cosine / math.sqrt(Q), sine / math.sqrt(Q)
    eye = np.eye(ROWS)
    small = np.zeros((2, Q, 2, Q))
    small[0, :, 0] = cosine
    small[0, :, 1] = sine
    small[1, :, 1] = cosine
    small[1, :, 0] = -sine
    second = np.einsum("pgqa,rs->gprqsa", small, eye).reshape(1024, 1024)
    small = np.zeros((2, Q, 2, Q))
    small[0, :, 0] = cosine
    small[0, :, 1] = -sine
    small[1, :, 1] = cosine
    small[1, :, 0] = sine
    third = np.einsum("paqg,rs->rpagqs", small, eye)
    third = third.reshape(4, 2, 2, Q, Q, 2, ROWS).transpose(0, 2, 1, 3, 4, 5, 6).reshape(1024, 1024)
    cosine, sine = angles(Q, P_SIZE, A)
    turned = np.stack([np.tile(part.T, (1, 2)) for part in (cosine, sine)]).astype(np.float32)
    straight = [np.tile(part, (2, 1)).reshape(128, 4, 128).transpose(1, 0, 2).reshape(512, 128) for part in (cosine, sine)]
    straight = np.concatenate([np.stack(straight), turned, turned, turned]).astype(np.float32)
    return (rounded(first), rounded(second), turned), (rounded(third), rounded(last), straight)


def pack_kernel(echo_ref, out_ref, echo, stage, arrived):
    low = lax.broadcasted_iota(jnp.int32, (8, 128), 1) < HALF
    copies = []
    for step in range(PACKS):
        rows = pl.ds(step * (512 // PACKS), 512 // PACKS)
        copies.append(pltpu.make_async_copy(echo_ref.at[:, rows, :], echo.at[:, rows, :], arrived.at[step]))
        copies[-1].start()
    for dest in range(64):
        if dest % (64 // PACKS) == 0:
            copies[dest // (64 // PACKS)].wait()
        for plane in range(2):
            rows = echo[plane, dest * ROWS : (dest + 1) * ROWS, :].astype(jnp.float32)
            for part in range(4):
                stage[pl.ds((dest * 8 + plane * 4 + part) * 8, 8), :] = rows[:, part * 128 : (part + 1) * 128]
        for pair in range(4):
            even = stage[pl.ds(dest * 64 + 2 * pair, 8, stride=8), :]
            odd = stage[pl.ds(dest * 64 + 2 * pair + 1, 8, stride=8), :]
            lower = jnp.where(low, even, pltpu.roll(odd, HALF, 1))
            upper = jnp.where(low, pltpu.roll(even, HALF, 1), odd)
            both = jnp.concatenate([lower, upper], axis=0).astype(jnp.bfloat16)
            out_ref[dest, :, pair * 128 : (pair + 1) * 128] = both


def pack(echoes):
    return pl.pallas_call(
        pack_kernel,
        in_specs=[pl.BlockSpec(memory_space=FAR)],
        out_specs=pl.BlockSpec(memory_space=NEAR),
        out_shape=jax.ShapeDtypeStruct((64, 16, 512), jnp.bfloat16),
        scratch_shapes=[
            pltpu.VMEM((2, 512, 512), jnp.bfloat16),
            pltpu.VMEM((4096, 128), jnp.float32),
            pltpu.SemaphoreType.DMA((PACKS,)),
        ],
        compiler_params=pltpu.CompilerParams(vmem_limit_bytes=53 * MIB),
        name="pack",
    )(echoes)


def fetch(source, target, arrived, steps):
    copies = []
    rows = source.shape[0] // steps
    for step in range(steps):
        span = pl.ds(step * rows, rows)
        copies.append(pltpu.make_async_copy(source.at[span], target.at[span], arrived.at[step]))
    return copies


def forward_kernel(
    x_ref, first_ref, second_ref, twist_ref, out_ref, first, second, twist, turned, sums, out, came, went
):
    lead = fetch(first_ref, first, came.at[0], 4)
    turns = fetch(twist_ref, twist, came.at[1], 1)
    follow = fetch(second_ref, second, came.at[2], 4)
    for copy in lead[:2] + turns:
        copy.start()
    later = [lead[2:3], lead[3:], follow[:2], follow[2:]]
    for chunk in range(4):
        lead[chunk].wait()
        for copy in later[chunk]:
            copy.start()
        sums[...] = jnp.dot(
            first[chunk * 256 : (chunk + 1) * 256, :], x_ref[...], preferred_element_type=jnp.float32
        )
        if chunk == 0:
            turns[0].wait()
        span = slice(chunk * 128, (chunk + 1) * 128)
        cosine, sine = twist[0, span, :], twist[1, span, :]
        for pair in range(4):
            lanes = slice(pair * 128, (pair + 1) * 128)
            real, imaginary = sums[:128, lanes], sums[128:, lanes]
            turned[span, pair * 128 : (pair + 1) * 128] = (real * cosine + imaginary * sine).astype(jnp.bfloat16)
            turned[span, 512 + pair * 128 : 640 + pair * 128] = (imaginary * cosine - real * sine).astype(
                jnp.bfloat16
            )
    sent = []
    for chunk in range(4):
        follow[chunk].wait()
        sums[...] = lax.dot_general(
            second[chunk * 256 : (chunk + 1) * 256, :],
            turned[...],
            (((1,), (1,)), ((), ())),
            preferred_element_type=jnp.float32,
        )
        span = slice(chunk * 16, (chunk + 1) * 16)
        for part in range(4):
            values = sums[:, part * 128 : (part + 1) * 128].astype(jnp.bfloat16)
            out[span, part] = values.reshape(16, 16, 128)
        rows = pl.ds(chunk * 16, 16)
        sent.append(pltpu.make_async_copy(out.at[rows], out_ref.at[rows], went.at[chunk]))
        sent[-1].start()
    for copy in sent:
        copy.wait()


def forward(x, first, second, twist):
    return pl.pallas_call(
        forward_kernel,
        out_shape=jax.ShapeDtypeStruct((64, 4, 16, 128), jnp.bfloat16),
        in_specs=[pl.BlockSpec(memory_space=NEAR)] + [pl.BlockSpec(memory_space=FAR)] * 3,
        out_specs=pl.BlockSpec(memory_space=FAR),
        scratch_shapes=[
            pltpu.VMEM((1024, 1024), jnp.bfloat16),
            pltpu.VMEM((1024, 1024), jnp.bfloat16),
            pltpu.VMEM((2, 512, 128), jnp.float32),
            pltpu.VMEM((512, 1024), jnp.bfloat16),
            pltpu.VMEM((256, 512), jnp.float32),
            pltpu.VMEM((64, 4, 16, 128), jnp.bfloat16),
            pltpu.SemaphoreType.DMA((3, 4)),
            pltpu.SemaphoreType.DMA((4,)),
        ],
        compiler_params=pltpu.CompilerParams(vmem_limit_bytes=51 * MIB),
        name="forward",
    )(x, first, second, twist)


def taps_kernel(band_ref, coef_ref, taps):
    lower = band_ref[1]
    width = band_ref[2]
    empty = jnp.zeros((TILE, TILE), jnp.bfloat16)
    taps[:TILE, 5 * TILE :] = empty
    taps[TILE:, :TILE] = empty
    for shift in range(WMAX):
        index = shift - HT - lower
        held = jnp.logical_and(index >= 0, index < width)
        weight = coef_ref[0, jnp.clip(index, 0, WMAX - 1)]
        scale = jnp.where(held, jnp.float32(1), jnp.float32(0))
        weight = (weight.astype(jnp.float32) * scale).astype(jnp.bfloat16)
        taps[:TILE, shift * TILE : (shift + 1) * TILE] = weight
        taps[TILE:, (shift + 1) * TILE : (shift + 2) * TILE] = weight


def tap_matrix(band, coef_table):
    return pl.pallas_call(
        taps_kernel,
        grid_spec=pltpu.PrefetchScalarGridSpec(
            num_scalar_prefetch=1,
            grid=(1,),
            in_specs=[pl.BlockSpec((1, WMAX, TILE, TILE), lambda i, band: (band[0], 0, 0, 0))],
            out_specs=pl.BlockSpec((256, 6 * TILE), lambda i, band: (0, 0)),
        ),
        out_shape=jax.ShapeDtypeStruct((256, 6 * TILE), jnp.bfloat16),
        compiler_params=pltpu.CompilerParams(vmem_limit_bytes=16 * MIB),
        cost_estimate=pl.CostEstimate(flops=2_000_000, bytes_accessed=600_000, transcendentals=0),
        name="taps",
    )(band, coef_table)


def migrate_kernel(spectrum_ref, taps, out_ref, padded, out, went):
    rim = jnp.zeros((HT * TILE, 2 * FB), jnp.bfloat16)
    padded[: HT * TILE, :] = rim
    padded[HT * TILE + R :, :] = rim
    for block in range(8):
        values = spectrum_ref[block * 32 : (block + 1) * 32].astype(jnp.float32)
        start = HT * TILE + block * 256
        for plane in range(2):
            rows = values[:, plane * ROWS : (plane + 1) * ROWS, :].reshape(256, FB)
            padded[start : start + 256, plane * FB : (plane + 1) * FB] = rows.astype(jnp.bfloat16)
    sent = []
    for block in range(8):
        moved = jnp.dot(
            taps[...], padded[block * 256 : block * 256 + 6 * TILE, :], preferred_element_type=jnp.float32
        )
        real = moved[:, :FB].reshape(32, ROWS, FB)
        imaginary = moved[:, FB:].reshape(32, ROWS, FB)
        out[block * 32 : (block + 1) * 32] = jnp.concatenate([real, imaginary], axis=1).astype(jnp.bfloat16)
        if block % 2 == 1:
            rows = pl.ds(block * 32 - 32, 64)
            sent.append(pltpu.make_async_copy(out.at[rows], out_ref.at[rows], went.at[block // 2]))
            sent[-1].start()
    for copy in sent:
        copy.wait()


def migrate(spectrum, taps):
    return pl.pallas_call(
        migrate_kernel,
        in_specs=[pl.BlockSpec(memory_space=NEAR)] * 2,
        out_specs=pl.BlockSpec(memory_space=FAR),
        scratch_shapes=[
            pltpu.VMEM((R + 2 * HT * TILE, 2 * FB), jnp.bfloat16),
            pltpu.VMEM((256, 16, 128), jnp.bfloat16),
            pltpu.SemaphoreType.DMA((4,)),
        ],
        out_shape=jax.ShapeDtypeStruct((256, 16, 128), jnp.bfloat16),
        compiler_params=pltpu.CompilerParams(vmem_limit_bytes=50 * MIB),
        name="migrate",
    )(spectrum, taps)


def rotor(turns):
    quarter = jnp.round(turns * 4.0)
    x = (turns - quarter * 0.25) * (2.0 * math.pi)
    square = x * x
    sine = x + x * square * (-1.0 / 6 + square * (1.0 / 120 + square * (-1.0 / 5040)))
    cosine = 1.0 + square * (-0.5 + square * (1.0 / 24 + square * (-1.0 / 720 + square * (1.0 / 40320))))
    count = quarter.astype(jnp.int32)
    swapped = (count & 1) == 1
    first = jnp.where(swapped, sine, cosine)
    second = jnp.where(swapped, cosine, sine)
    first = jnp.where(((count + 1) & 2) == 2, -first, first)
    second = jnp.where((count & 2) == 2, -second, second)
    return first, second


def phase_kernel(rate_ref, phase_ref):
    rate = rate_ref[...]
    lane = lax.broadcasted_iota(jnp.int32, (16, ROWS, FB), 2)
    step = lax.broadcasted_iota(jnp.int32, (16, ROWS, FB), 0)
    for chunk in range(4):
        for part in range(4):
            frequency = (step + chunk * 16) * P_SIZE + (lane + part * FB)
            signed = jnp.where(frequency >= A // 2, frequency - A, frequency).astype(jnp.float32)
            doppler = signed * (1.0 / A)
            cosine, sine = rotor(rate[None] * (doppler * doppler))
            phase_ref[0, chunk * 16 : (chunk + 1) * 16, part] = cosine
            phase_ref[1, chunk * 16 : (chunk + 1) * 16, part] = sine


def phases(rate):
    return pl.pallas_call(
        phase_kernel,
        out_shape=jax.ShapeDtypeStruct((2, 64, 4, ROWS, FB), jnp.float32),
        in_specs=[pl.BlockSpec(memory_space=NEAR)],
        out_specs=pl.BlockSpec(memory_space=NEAR),
        compiler_params=pltpu.CompilerParams(vmem_limit_bytes=16 * MIB),
        cost_estimate=pl.CostEstimate(flops=20_000_000, bytes_accessed=2_100_000, transcendentals=0),
        name="phases",
    )(rate)


def inverse_kernel(
    moved_ref,
    phase_ref,
    third_ref,
    last_ref,
    twist_ref,
    out_ref,
    third,
    last,
    twist,
    focused,
    turned,
    sums,
    stage,
    out,
    came,
    went,
):
    lead = fetch(third_ref, third, came.at[0], 4)
    turns = fetch(twist_ref.at[:2], twist, came.at[1], 1)
    follow = fetch(last_ref, last, came.at[2], 4)
    for copy in lead[:2] + turns:
        copy.start()
    later = [lead[2:3], lead[3:], follow[:2], follow[2:]]
    for chunk in range(4):
        for part in range(4):
            span = slice(chunk * 16, (chunk + 1) * 16)
            cosine, sine = phase_ref[0, span, part], phase_ref[1, span, part]
            values = moved_ref[span, part].astype(jnp.float32)
            real, imaginary = values[:, :ROWS, :], values[:, ROWS:, :]
            both = jnp.concatenate(
                [real * cosine + imaginary * sine, imaginary * cosine - real * sine], axis=1
            ).astype(jnp.bfloat16)
            focused[chunk * 256 : (chunk + 1) * 256, part * FB : (part + 1) * FB] = both.reshape(256, FB)
    for chunk in range(4):
        lead[chunk].wait()
        for copy in later[chunk]:
            copy.start()
        if chunk == 0:
            turns[0].wait()
        sums[...] = jnp.dot(
            third[chunk * 256 : (chunk + 1) * 256, :], focused[...], preferred_element_type=jnp.float32
        )
        span = slice(chunk * 128, (chunk + 1) * 128)
        for part in range(4):
            lanes = slice(part * 128, (part + 1) * 128)
            real, imaginary = sums[:128, lanes], sums[128:, lanes]
            cosine, sine = twist[0, lanes, :], twist[1, lanes, :]
            turned[span, part * 128 : (part + 1) * 128] = (real * cosine - imaginary * sine).astype(jnp.bfloat16)
            turned[span, 512 + part * 128 : 640 + part * 128] = (imaginary * cosine + real * sine).astype(
                jnp.bfloat16
            )
    low = lax.broadcasted_iota(jnp.int32, (128, 128), 1) < HALF
    sent = []
    for chunk in range(4):
        follow[chunk].wait()
        sums[...] = lax.dot_general(
            last[chunk * 256 : (chunk + 1) * 256, :],
            turned[...],
            (((1,), (1,)), ((), ())),
            preferred_element_type=jnp.float32,
        )
        for pair in range(4):
            even = sums[:128, pair * 128 : (pair + 1) * 128]
            odd = sums[128:, pair * 128 : (pair + 1) * 128]
            stage[chunk % 2, pl.ds(2 * pair, 128, stride=8), :] = jnp.where(low, even, pltpu.roll(odd, HALF, 1))
            stage[chunk % 2, pl.ds(2 * pair + 1, 128, stride=8), :] = jnp.where(low, pltpu.roll(even, HALF, 1), odd)
        plane, base = chunk // 2, (chunk % 2) * 128
        for group in range(128):
            out[plane, :, (base + group) * 128 : (base + group + 1) * 128] = stage[
                chunk % 2, group * 8 : (group + 1) * 8, :
            ].astype(jnp.bfloat16)
        lanes = pl.ds(base * 128, A // 2)
        sent.append(pltpu.make_async_copy(out.at[plane, :, lanes], out_ref.at[plane, :, lanes], went.at[chunk]))
        sent[-1].start()
    for copy in sent:
        copy.wait()


def inverse(moved, phase, third, last, twist):
    return pl.pallas_call(
        inverse_kernel,
        out_shape=jax.ShapeDtypeStruct((2, ROWS, A), jnp.bfloat16),
        in_specs=[pl.BlockSpec(memory_space=NEAR)] * 2 + [pl.BlockSpec(memory_space=FAR)] * 3,
        out_specs=pl.BlockSpec(memory_space=FAR),
        scratch_shapes=[
            pltpu.VMEM((1024, 1024), jnp.bfloat16),
            pltpu.VMEM((1024, 1024), jnp.bfloat16),
            pltpu.VMEM((2, 512, 128), jnp.float32),
            pltpu.VMEM((1024, 512), jnp.bfloat16),
            pltpu.VMEM((512, 1024), jnp.bfloat16),
            pltpu.VMEM((256, 512), jnp.float32),
            pltpu.VMEM((2, 1024, 128), jnp.float32),
            pltpu.VMEM((2, ROWS, A), jnp.bfloat16),
            pltpu.SemaphoreType.DMA((3, 4)),
            pltpu.SemaphoreType.DMA((4,)),
        ],
        compiler_params=pltpu.CompilerParams(vmem_limit_bytes=50 * MIB),
        name="inverse",
    )(moved, phase, third, last, twist)


def body(echoes, coef_table, kern_id, band_lo, band_width, rate):
    ahead, behind = tables()
    az = lax.axis_index("az")
    block = lax.axis_index("rg") * lax.axis_size("az") + az
    band = jnp.stack([kern_id[block], band_lo[block], band_width[block]])
    rates = jnp.broadcast_to(lax.dynamic_slice(rate, (az * ROWS,), (ROWS,))[:, None], (ROWS, FB))
    piece = lax.all_to_all(pack(echoes), "az", 0, 0, tiled=True)
    spectrum = forward(piece.reshape(1024, 512), *ahead)
    spectrum = lax.all_to_all(spectrum.reshape(256, 16, 128), ("rg", "az"), 0, 0, tiled=True)
    moved = migrate(spectrum, tap_matrix(band, coef_table))
    moved = lax.all_to_all(moved, ("rg", "az"), 0, 0, tiled=True)
    return inverse(moved.reshape(64, 4, 16, 128), phases(rates), *behind)


def solution(mesh):
    in_specs = (P(None, "rg", "az"), P(), P(), P(), P(), P("rg"))
    out_specs = P(None, ("rg", "az"), None)
    return jax.shard_map(body, mesh=mesh, in_specs=in_specs, out_specs=out_specs, check_vma=False)
```

time: 140 us -> 138 us (0.986)
  Pallas kernels: 14.1 us -> 19.5 us
  local copies, waits for them, and re-layouts: 7.9 us -> 2.75 us
  waiting for transfers between devices: 59.8 us -> 57.2 us
    unnamed x24 -> x10, local copies, waits for them, and re-layouts: 5.26 us -> 0.03 us
    pallas_call x2 -> x4, Pallas kernels: 3.43 us -> 6.86 us  [the longest x1 3.05 us: pack(): pl.pallas_call(pack_kernel, in_specs=[pl.BlockSpec(memory_space=FAR)], ou...]
    all_to_all x1, waiting for transfers between devices: 31 us -> 29.3 us  [body(): moved = lax.all_to_all(moved, ('rg', 'az'), 0, 0, tiled=True)]
  transfers between devices with their start and end apart: 2 -> 2, of which waited for: 2 -> 2; matrix products, arithmetic and copies ran while one was open for 3% -> 3% of each run, Pallas kernels for 0% -> 1%
where the time goes in v2:
time: 138 us
  waiting for transfers between devices  57.2 us (41%)
  blocking collectives  41.6 us (30%)
  Pallas kernels  19.5 us (14%)
  starting transfers between devices  14.2 us (10%)
  local copies, waits for them, and re-layouts  2.75 us (2%)
  other arithmetic  2.01 us (1%)
    all_to_all x1, blocking collectives, body(): piece = lax.all_to_all(pack(echoes), 'az', 0, 0, tiled=True)  41.6 us
    all_to_all x1, waiting for transfers between devices, body(): moved = lax.all_to_all(moved, ('rg', 'az'), 0, 0, tiled=True)  29.3 us
    all_to_all x1, waiting for transfers between devices, body(): lax.all_to_all(spectrum.reshape(256, 16, 128), ('rg', 'az'), 0, 0, tiled=...  27.9 us
    all_to_all x1, starting transfers between devices, body(): lax.all_to_all(spectrum.reshape(256, 16, 128), ('rg', 'az'), 0, 0, tiled=...  8.87 us
    pallas_call x1, Pallas kernels, inverse(): pl.pallas_call(inverse_kernel, out_shape=jax.ShapeDtypeStruct((2, ROWS, A...  6.73 us
    pallas_call x1, Pallas kernels, forward(): pl.pallas_call(forward_kernel, out_shape=jax.ShapeDtypeStruct((64, 4, 16,...  5.95 us
    all_to_all x1, starting transfers between devices, body(): moved = lax.all_to_all(moved, ('rg', 'az'), 0, 0, tiled=True)  5.37 us
    pallas_call x1, Pallas kernels, pack(): pl.pallas_call(pack_kernel, in_specs=[pl.BlockSpec(memory_space=FAR)], ou...  3.05 us
  transfers between devices with their start and end apart: 2, of which 2 were waited for; matrix products, arithmetic and copies ran while one was open for 3% of the time, Pallas kernels for 1%

profile of v2, /device:TPU:1, one launch (start us, length us, event | category | flops | bytes accessed | tf_op | source)
XLA Modules:
  0.0 137.6 jit_solution(16249784713545129894)
XLA Ops:
  0.0 3.0 %pack.1 = bf16[64,16,512]{2,1,0:T(8,128)(2,1)} custom-call(bf16[2,512,512]{2,1,0:T(8,128)(2,1)} %echo_ref.1), custom_call_target="tpu_custom_call" | custom-call | tf_op jit(solution)/shard_map/pack/pallas_call | solution.py:103
  3.1 41.6 %all_to_all.15 = bf16[64,16,512]{2,1,0:T(8,128)(2,1)S(1)} all-to-all(bf16[64,16,512]{2,1,0:T(8,128)(2,1)} %pack.1), channel_id=1, replica_groups=mesh['az'=64,'rg'=4] {'az'}, dimensions={0} | all-to-all | bytes 2097152 | tf_op jit(solution)/shard_map/all_to_all | solution.py:418
  44.6 0.0 copy-done.1
  44.6 5.9 %forward.1 = bf16[64,4,16,128]{3,2,1,0:T(8,128)(2,1)} custom-call(bf16[1024,512]{1,0:T(8,128)(2,1)S(1)} %bitcast.4, bf16[1024,1024]{1,0:T(8,128)(2,1)} %constant.31.clone.first_ref, bf16[1024,1024]{1,0:T(8,128)(2,1)} %constant.32.clone.second_ref, f32[2,512,128]{2,1,0:T(8,128)S(1)} %copy-done.1), custom_call_target="tpu_custom_call" | custom-call | tf_op jit(solution)/shard_map/forward/pallas_call | solution.py:175
  50.6 0.0 copy-start.2
  50.6 0.0 copy-start.3
  50.6 0.0 copy-start.4
  50.6 0.0 copy-start
  50.6 8.9 %all-to-all-start.1 = ((bf16[256,16,128]{2,1,0:T(8,128)(2,1)}), bf16[256,16,128]{2,1,0:T(8,128)(2,1)S(1)}, u32[]{:S(2)}, u32[]{:S(2)}) async-start(bf16[256,16,128]{2,1,0:T(8,128)(2,1)} %bitcast.1), calls=%async_computation.1 | async-start | bytes 2097152 | tf_op jit(solution)/shard_map/all_to_all | solution.py:420
  59.5 0.0 copy-done.2
  59.5 0.7 dynamic_slice.14
  60.2 0.6 dynamic_slice.13
  60.8 0.0 copy-done.4
  60.8 0.6 dynamic_slice.12
  61.4 2.0 %pad_add_fusion.band_ref = s32[3]{0:T(128)S(1)} fusion(s32[1]{0:T(128)} %dynamic_slice.14, s32[1]{0:T(128)} %dynamic_slice.13, s32[1]{0:T(128)} %dynamic_slice.12), kind=kLoop, calls=%fused_computation | loop fusion | flops 6 | bytes 24 | tf_op jit(solution)/shard_map/stack | solution.py:416
  63.4 0.6 taps.1
  64.0 27.9 %all-to-all-done.1.spectrum_ref = bf16[256,16,128]{2,1,0:T(8,128)(2,1)S(1)} async-done(((bf16[256,16,128]{2,1,0:T(8,128)(2,1)}), bf16[256,16,128]{2,1,0:T(8,128)(2,1)S(1)}, u32[]{:S(2)}, u32[]{:S(2)}) %all-to-all-start.1) | async-done | bytes 1048608 | tf_op jit(solution)/shard_map/all_to_all | solution.py:420
  91.9 1.8 %migrate.1 = bf16[256,16,128]{2,1,0:T(8,128)(2,1)} custom-call(bf16[256,16,128]{2,1,0:T(8,128)(2,1)S(1)} %all-to-all-done.1.spectrum_ref, bf16[256,768]{1,0:T(8,128)(2,1)S(1)} %taps.1), custom_call_target="tpu_custom_call" | custom-call | tf_op jit(solution)/shard_map/migrate/pallas_call | solution.py:254
  93.7 5.4 %all-to-all-start.2 = ((bf16[256,16,128]{2,1,0:T(8,128)(2,1)}), bf16[256,16,128]{2,1,0:T(8,128)(2,1)S(1)}, u32[]{:S(2)}, u32[]{:S(2)}) async-start(bf16[256,16,128]{2,1,0:T(8,128)(2,1)} %migrate.1), calls=%async_computation.2 | async-start | bytes 2097152 | tf_op jit(solution)/shard_map/all_to_all | solution.py:422
  99.1 0.8 dynamic_slice.15
  99.8 0.1 broadcast_in_dim.2.rate_ref
  99.9 1.5 %phases.1.phase_ref = f32[2,64,4,8,128]{4,3,2,1,0:T(8,128)S(1)} custom-call(f32[8,128]{1,0:T(8,128)S(1)} %broadcast_in_dim.2.rate_ref), custom_call_target="tpu_custom_call" | custom-call | flops 20000000 | bytes 2100000 | tf_op jit(solution)/shard_map/phases/pallas_call | solution.py:299
  101.4 29.3 %all-to-all-done.2 = bf16[256,16,128]{2,1,0:T(8,128)(2,1)S(1)} async-done(((bf16[256,16,128]{2,1,0:T(8,128)(2,1)}), bf16[256,16,128]{2,1,0:T(8,128)(2,1)S(1)}, u32[]{:S(2)}, u32[]{:S(2)}) %all-to-all-start.2) | async-done | bytes 1048608 | tf_op jit(solution)/shard_map/all_to_all | solution.py:422
  130.7 6.7 %inverse.1 = bf16[2,8,32768]{2,1,0:T(8,128)(2,1)} custom-call(bf16[64,4,16,128]{3,2,1,0:T(8,128)(2,1)S(1)} %bitcast.3, f32[2,64,4,8,128]{4,3,2,1,0:T(8,128)S(1)} %phases.1.phase_ref, bf16[1024,1024]{1,0:T(8,128)(2,1)} %constant.34.clone.third_ref, bf16[1024,1024]{1,0:T(8,128)(2,1)} %constant.35.clone.last_ref, f32[8,512,128]{2,1,0:T(8,128)} %constant.36.clone.twist_ref), custom_call_target="tpu_custom_call" | custom-call | tf_op jit(solution)/shard_map/inverse/pallas_call | solution.py:390
  (3 shorter events, 0.0 us)
Async XLA Ops:
  0.0 44.6 %copy-start.1 = (f32[2,512,128]{2,1,0:T(8,128)S(1)}, f32[2,512,128]{2,1,0:T(8,128)}, u32[]{:S(2)}) copy-start(f32[2,512,128]{2,1,0:T(8,128)} %constant.33.clone.twist_ref) | copy-start | bytes 1572868
  50.6 8.9 %copy-start.2 = (s32[256]{0:T(256)S(1)}, s32[256]{0:T(256)}, u32[]{:S(2)}) copy-start(s32[256]{0:T(256)} %param.16) | copy-start | bytes 3076
  50.6 9.6 %copy-start.3 = (s32[256]{0:T(256)S(1)}, s32[256]{0:T(256)}, u32[]{:S(2)}) copy-start(s32[256]{0:T(256)} %param.15) | copy-start | bytes 3076
  50.6 10.2 %copy-start.4 = (s32[256]{0:T(256)S(1)}, s32[256]{0:T(256)}, u32[]{:S(2)}) copy-start(s32[256]{0:T(256)} %param.14) | copy-start | bytes 3076
  50.6 12.8 %copy-start = (bf16[8,5,128,128]{3,2,1,0:T(8,128)(2,1)S(1)}, bf16[8,5,128,128]{3,2,1,0:T(8,128)(2,1)}, u32[]{:S(2)}) copy-start(bf16[8,5,128,128]{3,2,1,0:T(8,128)(2,1)} %coef_ref.1) | copy-start | bytes 3932164
  50.6 41.3 %all-to-all-start.1 = ((bf16[256,16,128]{2,1,0:T(8,128)(2,1)}), bf16[256,16,128]{2,1,0:T(8,128)(2,1)S(1)}, u32[]{:S(2)}, u32[]{:S(2)}) async-start(bf16[256,16,128]{2,1,0:T(8,128)(2,1)} %bitcast.1), calls=%async_computation.1 | async-start | bytes 2097152 | tf_op jit(solution)/shard_map/all_to_all | solution.py:420
  93.7 37.0 %all-to-all-start.2 = ((bf16[256,16,128]{2,1,0:T(8,128)(2,1)}), bf16[256,16,128]{2,1,0:T(8,128)(2,1)S(1)}, u32[]{:S(2)}, u32[]{:S(2)}) async-start(bf16[256,16,128]{2,1,0:T(8,128)(2,1)} %migrate.1), calls=%async_computation.2 | async-start | bytes 2097152 | tf_op jit(solution)/shard_map/all_to_all | solution.py:422

commit v3 on v2

--- a/solution.py
+++ b/solution.py
@@ -73,7 +73,7 @@
     turned = np.stack([np.tile(part.T, (1, 2)) for part in (cosine, sine)]).astype(np.float32)
     straight = [np.tile(part, (2, 1)).reshape(128, 4, 128).transpose(1, 0, 2).reshape(512, 128) for part in (cosine, sine)]
     straight = np.concatenate([np.stack(straight), turned, turned, turned]).astype(np.float32)
-    return (rounded(first), rounded(second), turned), (rounded(third), rounded(last), straight)
+    return (rounded(first), turned, rounded(second)), (rounded(third), rounded(last), straight)
 
 
 def pack_kernel(echo_ref, out_ref, echo, stage, arrived):
@@ -110,7 +110,7 @@
             pltpu.VMEM((4096, 128), jnp.float32),
             pltpu.SemaphoreType.DMA((PACKS,)),
         ],
-        compiler_params=pltpu.CompilerParams(vmem_limit_bytes=53 * MIB),
+        compiler_params=pltpu.CompilerParams(vmem_limit_bytes=52 * MIB),
         name="pack",
     )(echoes)
 
@@ -125,23 +125,15 @@
 
 
 def forward_kernel(
-    x_ref, first_ref, second_ref, twist_ref, out_ref, first, second, twist, turned, sums, out, came, went
+    x_ref, first, twist, second_ref, out_ref, second, turned, sums, out, came, went
 ):
-    lead = fetch(first_ref, first, came.at[0], 4)
-    turns = fetch(twist_ref, twist, came.at[1], 1)
-    follow = fetch(second_ref, second, came.at[2], 4)
-    for copy in lead[:2] + turns:
+    follow = fetch(second_ref, second, came, 4)
+    for copy in follow:
         copy.start()
-    later = [lead[2:3], lead[3:], follow[:2], follow[2:]]
-    for chunk in range(4):
-        lead[chunk].wait()
-        for copy in later[chunk]:
-            copy.start()
+    for chunk in range(4):
         sums[...] = jnp.dot(
             first[chunk * 256 : (chunk + 1) * 256, :], x_ref[...], preferred_element_type=jnp.float32
         )
-        if chunk == 0:
-            turns[0].wait()
         span = slice(chunk * 128, (chunk + 1) * 128)
         cosine, sine = twist[0, span, :], twist[1, span, :]
         for pair in range(4):
@@ -171,25 +163,23 @@
         copy.wait()
 
 
-def forward(x, first, second, twist):
+def forward(x, first, twist, second):
     return pl.pallas_call(
         forward_kernel,
         out_shape=jax.ShapeDtypeStruct((64, 4, 16, 128), jnp.bfloat16),
-        in_specs=[pl.BlockSpec(memory_space=NEAR)] + [pl.BlockSpec(memory_space=FAR)] * 3,
+        in_specs=[pl.BlockSpec(memory_space=NEAR)] * 3 + [pl.BlockSpec(memory_space=FAR)],
         out_specs=pl.BlockSpec(memory_space=FAR),
         scratch_shapes=[
             pltpu.VMEM((1024, 1024), jnp.bfloat16),
-            pltpu.VMEM((1024, 1024), jnp.bfloat16),
-            pltpu.VMEM((2, 512, 128), jnp.float32),
             pltpu.VMEM((512, 1024), jnp.bfloat16),
             pltpu.VMEM((256, 512), jnp.float32),
             pltpu.VMEM((64, 4, 16, 128), jnp.bfloat16),
-            pltpu.SemaphoreType.DMA((3, 4)),
+            pltpu.SemaphoreType.DMA((4,)),
             pltpu.SemaphoreType.DMA((4,)),
         ],
-        compiler_params=pltpu.CompilerParams(vmem_limit_bytes=51 * MIB),
+        compiler_params=pltpu.CompilerParams(vmem_limit_bytes=49 * MIB),
         name="forward",
-    )(x, first, second, twist)
+    )(x, first, twist, second)
 
 
 def taps_kernel(band_ref, coef_ref, taps):
@@ -328,9 +318,8 @@
     lead = fetch(third_ref, third, came.at[0], 4)
     turns = fetch(twist_ref.at[:2], twist, came.at[1], 1)
     follow = fetch(last_ref, last, came.at[2], 4)
-    for copy in lead[:2] + turns:
+    for copy in lead[:1] + turns + lead[1:] + follow:
         copy.start()
-    later = [lead[2:3], lead[3:], follow[:2], follow[2:]]
     for chunk in range(4):
         for part in range(4):
             span = slice(chunk * 16, (chunk + 1) * 16)
@@ -343,8 +332,6 @@
             focused[chunk * 256 : (chunk + 1) * 256, part * FB : (part + 1) * FB] = both.reshape(256, FB)
     for chunk in range(4):
         lead[chunk].wait()
-        for copy in later[chunk]:
-            copy.start()
         if chunk == 0:
             turns[0].wait()
         sums[...] = jnp.dot(

time: 138 us -> 135 us (0.978)
  Pallas kernels: 19.5 us -> 16.4 us
    pallas_call x1, Pallas kernels: 5.95 us -> 3.99 us  [forward(): pl.pallas_call(forward_kernel, out_shape=jax.ShapeDtypeStruct((64, 4, 16,...]
  transfers between devices with their start and end apart: 2 -> 2, of which waited for: 2 -> 2; matrix products, arithmetic and copies ran while one was open for 3% -> 3% of each run, Pallas kernels for 1% -> 2%
where the time goes in v3:
time: 135 us; the launch traced here: 134 us
  waiting for transfers between devices  57.3 us (42%)
  blocking collectives  41.3 us (31%)
  Pallas kernels  16.4 us (12%)
  starting transfers between devices  14.2 us (11%)
  local copies, waits for them, and re-layouts  2.75 us (2%)
  other arithmetic  1.95 us (1%)
    all_to_all x1, blocking collectives, body(): piece = lax.all_to_all(pack(echoes), 'az', 0, 0, tiled=True)  41.3 us
    all_to_all x1, waiting for transfers between devices, body(): moved = lax.all_to_all(moved, ('rg', 'az'), 0, 0, tiled=True)  29.3 us
    all_to_all x1, waiting for transfers between devices, body(): lax.all_to_all(spectrum.reshape(256, 16, 128), ('rg', 'az'), 0, 0, tiled=...  28 us
    all_to_all x1, starting transfers between devices, body(): lax.all_to_all(spectrum.reshape(256, 16, 128), ('rg', 'az'), 0, 0, tiled=...  8.87 us
    pallas_call x1, Pallas kernels, inverse(): pl.pallas_call(inverse_kernel, out_shape=jax.ShapeDtypeStruct((2, ROWS, A...  6.42 us
    all_to_all x1, starting transfers between devices, body(): moved = lax.all_to_all(moved, ('rg', 'az'), 0, 0, tiled=True)  5.37 us
    pallas_call x1, Pallas kernels, forward(): pl.pallas_call(forward_kernel, out_shape=jax.ShapeDtypeStruct((64, 4, 16,...  3.99 us
  transfers between devices with their start and end apart: 2, of which 2 were waited for; matrix products, arithmetic and copies ran while one was open for 3% of the time, Pallas kernels for 2%

profile of v3, /device:TPU:1, one launch (start us, length us, event | category | flops | bytes accessed | tf_op | source)
XLA Modules:
  0.0 134.3 jit_solution(12870833325408438436)
XLA Ops:
  0.0 2.2 %pack.1 = bf16[64,16,512]{2,1,0:T(8,128)(2,1)S(1)} custom-call(bf16[2,512,512]{2,1,0:T(8,128)(2,1)} %echo_ref.1), custom_call_target="tpu_custom_call" | custom-call | tf_op jit(solution)/shard_map/pack/pallas_call | solution.py:103
  2.2 41.3 %all_to_all.15 = bf16[64,16,512]{2,1,0:T(8,128)(2,1)S(1)} all-to-all(bf16[64,16,512]{2,1,0:T(8,128)(2,1)S(1)} %pack.1), channel_id=1, replica_groups=mesh['az'=64,'rg'=4] {'az'}, dimensions={0} | all-to-all | bytes 2097152 | tf_op jit(solution)/shard_map/all_to_all | solution.py:405
  43.5 0.0 copy-done
  43.5 0.0 copy-done.2
  43.5 4.0 %forward.1 = bf16[64,4,16,128]{3,2,1,0:T(8,128)(2,1)} custom-call(bf16[1024,512]{1,0:T(8,128)(2,1)S(1)} %bitcast.4, bf16[1024,1024]{1,0:T(8,128)(2,1)S(1)} %copy-done, f32[2,512,128]{2,1,0:T(8,128)S(1)} %copy-done.2, bf16[1024,1024]{1,0:T(8,128)(2,1)} %constant.33.clone.second_ref), custom_call_target="tpu_custom_call" | custom-call | tf_op jit(solution)/shard_map/forward/pallas_call | solution.py:167
  47.5 0.0 copy-start.3
  47.5 0.0 copy-start.4
  47.6 0.0 copy-start.5
  47.6 0.0 copy-start.1
  47.6 8.9 %all-to-all-start.1 = ((bf16[256,16,128]{2,1,0:T(8,128)(2,1)}), bf16[256,16,128]{2,1,0:T(8,128)(2,1)S(1)}, u32[]{:S(2)}, u32[]{:S(2)}) async-start(bf16[256,16,128]{2,1,0:T(8,128)(2,1)} %bitcast.1), calls=%async_computation.1 | async-start | bytes 2097152 | tf_op jit(solution)/shard_map/all_to_all | solution.py:407
  56.5 0.6 dynamic_slice.14
  57.1 0.6 dynamic_slice.13
  57.7 0.0 copy-done.5
  57.7 0.6 dynamic_slice.12
  58.4 2.0 %pad_add_fusion.band_ref = s32[3]{0:T(128)S(1)} fusion(s32[1]{0:T(128)} %dynamic_slice.14, s32[1]{0:T(128)} %dynamic_slice.13, s32[1]{0:T(128)} %dynamic_slice.12), kind=kLoop, calls=%fused_computation | loop fusion | flops 6 | bytes 24 | tf_op jit(solution)/shard_map/stack | solution.py:403
  60.3 0.6 taps.1
  60.9 28.0 %all-to-all-done.1.spectrum_ref = bf16[256,16,128]{2,1,0:T(8,128)(2,1)S(1)} async-done(((bf16[256,16,128]{2,1,0:T(8,128)(2,1)}), bf16[256,16,128]{2,1,0:T(8,128)(2,1)S(1)}, u32[]{:S(2)}, u32[]{:S(2)}) %all-to-all-start.1) | async-done | bytes 1048608 | tf_op jit(solution)/shard_map/all_to_all | solution.py:407
  88.9 1.8 %migrate.1 = bf16[256,16,128]{2,1,0:T(8,128)(2,1)} custom-call(bf16[256,16,128]{2,1,0:T(8,128)(2,1)S(1)} %all-to-all-done.1.spectrum_ref, bf16[256,768]{1,0:T(8,128)(2,1)S(1)} %taps.1), custom_call_target="tpu_custom_call" | custom-call | tf_op jit(solution)/shard_map/migrate/pallas_call | solution.py:244
  90.7 5.4 %all-to-all-start.2 = ((bf16[256,16,128]{2,1,0:T(8,128)(2,1)}), bf16[256,16,128]{2,1,0:T(8,128)(2,1)S(1)}, u32[]{:S(2)}, u32[]{:S(2)}) async-start(bf16[256,16,128]{2,1,0:T(8,128)(2,1)} %migrate.1), calls=%async_computation.2 | async-start | bytes 2097152 | tf_op jit(solution)/shard_map/all_to_all | solution.py:409
  96.1 0.8 dynamic_slice.15
  96.8 0.1 broadcast_in_dim.2.rate_ref
  96.9 1.5 %phases.1.phase_ref = f32[2,64,4,8,128]{4,3,2,1,0:T(8,128)S(1)} custom-call(f32[8,128]{1,0:T(8,128)S(1)} %broadcast_in_dim.2.rate_ref), custom_call_target="tpu_custom_call" | custom-call | flops 20000000 | bytes 2100000 | tf_op jit(solution)/shard_map/phases/pallas_call | solution.py:289
  98.4 29.3 %all-to-all-done.2 = bf16[256,16,128]{2,1,0:T(8,128)(2,1)S(1)} async-done(((bf16[256,16,128]{2,1,0:T(8,128)(2,1)}), bf16[256,16,128]{2,1,0:T(8,128)(2,1)S(1)}, u32[]{:S(2)}, u32[]{:S(2)}) %all-to-all-start.2) | async-done | bytes 1048608 | tf_op jit(solution)/shard_map/all_to_all | solution.py:409
  127.7 6.4 %inverse.1 = bf16[2,8,32768]{2,1,0:T(8,128)(2,1)} custom-call(bf16[64,4,16,128]{3,2,1,0:T(8,128)(2,1)S(1)} %bitcast.3, f32[2,64,4,8,128]{4,3,2,1,0:T(8,128)S(1)} %phases.1.phase_ref, bf16[1024,1024]{1,0:T(8,128)(2,1)} %constant.34.clone.third_ref, bf16[1024,1024]{1,0:T(8,128)(2,1)} %constant.35.clone.last_ref, f32[8,512,128]{2,1,0:T(8,128)} %constant.36.clone.twist_ref), custom_call_target="tpu_custom_call" | custom-call | tf_op jit(solution)/shard_map/inverse/pallas_call | solution.py:377
  (5 shorter events, 0.0 us)
Async XLA Ops:
  0.0 43.5 %copy-start = (bf16[1024,1024]{1,0:T(8,128)(2,1)S(1)}, bf16[1024,1024]{1,0:T(8,128)(2,1)}, u32[]{:S(2)}) copy-start(bf16[1024,1024]{1,0:T(8,128)(2,1)} %constant.31.clone.first) | copy-start | bytes 6291460
  0.0 43.5 %copy-start.2 = (f32[2,512,128]{2,1,0:T(8,128)S(1)}, f32[2,512,128]{2,1,0:T(8,128)}, u32[]{:S(2)}) copy-start(f32[2,512,128]{2,1,0:T(8,128)} %constant.32.clone.twist) | copy-start | bytes 1572868
  47.5 8.9 %copy-start.3 = (s32[256]{0:T(256)S(1)}, s32[256]{0:T(256)}, u32[]{:S(2)}) copy-start(s32[256]{0:T(256)} %param.16) | copy-start | bytes 3076
  47.5 9.6 %copy-start.4 = (s32[256]{0:T(256)S(1)}, s32[256]{0:T(256)}, u32[]{:S(2)}) copy-start(s32[256]{0:T(256)} %param.15) | copy-start | bytes 3076
  47.6 10.2 %copy-start.5 = (s32[256]{0:T(256)S(1)}, s32[256]{0:T(256)}, u32[]{:S(2)}) copy-start(s32[256]{0:T(256)} %param.14) | copy-start | bytes 3076
  47.6 12.8 %copy-start.1 = (bf16[8,5,128,128]{3,2,1,0:T(8,128)(2,1)S(1)}, bf16[8,5,128,128]{3,2,1,0:T(8,128)(2,1)}, u32[]{:S(2)}) copy-start(bf16[8,5,128,128]{3,2,1,0:T(8,128)(2,1)} %coef_ref.1) | copy-start | bytes 3932164
  47.6 41.3 %all-to-all-start.1 = ((bf16[256,16,128]{2,1,0:T(8,128)(2,1)}), bf16[256,16,128]{2,1,0:T(8,128)(2,1)S(1)}, u32[]{:S(2)}, u32[]{:S(2)}) async-start(bf16[256,16,128]{2,1,0:T(8,128)(2,1)} %bitcast.1), calls=%async_computation.1 | async-start | bytes 2097152 | tf_op jit(solution)/shard_map/all_to_all | solution.py:407
  90.7 37.0 %all-to-all-start.2 = ((bf16[256,16,128]{2,1,0:T(8,128)(2,1)}), bf16[256,16,128]{2,1,0:T(8,128)(2,1)S(1)}, u32[]{:S(2)}, u32[]{:S(2)}) async-start(bf16[256,16,128]{2,1,0:T(8,128)(2,1)} %migrate.1), calls=%async_computation.2 | async-start | bytes 2097152 | tf_op jit(solution)/shard_map/all_to_all | solution.py:409

commit v4 on v3

--- a/solution.py
+++ b/solution.py
@@ -127,26 +127,26 @@
 def forward_kernel(
     x_ref, first, twist, second_ref, out_ref, second, turned, sums, out, came, went
 ):
-    follow = fetch(second_ref, second, came, 4)
+    follow = fetch(second_ref, second, came, 1)
     for copy in follow:
         copy.start()
     for chunk in range(4):
-        sums[...] = jnp.dot(
+        sums[chunk % 2] = jnp.dot(
             first[chunk * 256 : (chunk + 1) * 256, :], x_ref[...], preferred_element_type=jnp.float32
         )
         span = slice(chunk * 128, (chunk + 1) * 128)
         cosine, sine = twist[0, span, :], twist[1, span, :]
         for pair in range(4):
             lanes = slice(pair * 128, (pair + 1) * 128)
-            real, imaginary = sums[:128, lanes], sums[128:, lanes]
+            real, imaginary = sums[chunk % 2, :128, lanes], sums[chunk % 2, 128:, lanes]
             turned[span, pair * 128 : (pair + 1) * 128] = (real * cosine + imaginary * sine).astype(jnp.bfloat16)
             turned[span, 512 + pair * 128 : 640 + pair * 128] = (imaginary * cosine - real * sine).astype(
                 jnp.bfloat16
             )
+    follow[0].wait()
     sent = []
     for chunk in range(4):
-        follow[chunk].wait()
-        sums[...] = lax.dot_general(
+        sums[chunk % 2] = lax.dot_general(
             second[chunk * 256 : (chunk + 1) * 256, :],
             turned[...],
             (((1,), (1,)), ((), ())),
@@ -154,11 +154,12 @@
         )
         span = slice(chunk * 16, (chunk + 1) * 16)
         for part in range(4):
-            values = sums[:, part * 128 : (part + 1) * 128].astype(jnp.bfloat16)
+            values = sums[chunk % 2, :, part * 128 : (part + 1) * 128].astype(jnp.bfloat16)
             out[span, part] = values.reshape(16, 16, 128)
-        rows = pl.ds(chunk * 16, 16)
-        sent.append(pltpu.make_async_copy(out.at[rows], out_ref.at[rows], went.at[chunk]))
-        sent[-1].start()
+        if chunk % 2 == 1:
+            rows = pl.ds(chunk * 16 - 16, 32)
+            sent.append(pltpu.make_async_copy(out.at[rows], out_ref.at[rows], went.at[chunk // 2]))
+            sent[-1].start()
     for copy in sent:
         copy.wait()
 
@@ -172,10 +173,10 @@
         scratch_shapes=[
             pltpu.VMEM((1024, 1024), jnp.bfloat16),
             pltpu.VMEM((512, 1024), jnp.bfloat16),
-            pltpu.VMEM((256, 512), jnp.float32),
+            pltpu.VMEM((2, 256, 512), jnp.float32),
             pltpu.VMEM((64, 4, 16, 128), jnp.bfloat16),
-            pltpu.SemaphoreType.DMA((4,)),
-            pltpu.SemaphoreType.DMA((4,)),
+            pltpu.SemaphoreType.DMA((1,)),
+            pltpu.SemaphoreType.DMA((2,)),
         ],
         compiler_params=pltpu.CompilerParams(vmem_limit_bytes=49 * MIB),
         name="forward",
@@ -315,10 +316,10 @@
     came,
     went,
 ):
-    lead = fetch(third_ref, third, came.at[0], 4)
+    lead = fetch(third_ref, third, came.at[0], 1)
     turns = fetch(twist_ref.at[:2], twist, came.at[1], 1)
-    follow = fetch(last_ref, last, came.at[2], 4)
-    for copy in lead[:1] + turns + lead[1:] + follow:
+    follow = fetch(last_ref, last, came.at[2], 1)
+    for copy in lead + turns + follow:
         copy.start()
     for chunk in range(4):
         for part in range(4):
@@ -330,35 +331,34 @@
                 [real * cosine + imaginary * sine, imaginary * cosine - real * sine], axis=1
             ).astype(jnp.bfloat16)
             focused[chunk * 256 : (chunk + 1) * 256, part * FB : (part + 1) * FB] = both.reshape(256, FB)
-    for chunk in range(4):
-        lead[chunk].wait()
-        if chunk == 0:
-            turns[0].wait()
-        sums[...] = jnp.dot(
+    lead[0].wait()
+    turns[0].wait()
+    for chunk in range(4):
+        sums[chunk % 2] = jnp.dot(
             third[chunk * 256 : (chunk + 1) * 256, :], focused[...], preferred_element_type=jnp.float32
         )
         span = slice(chunk * 128, (chunk + 1) * 128)
         for part in range(4):
             lanes = slice(part * 128, (part + 1) * 128)
-            real, imaginary = sums[:128, lanes], sums[128:, lanes]
+            real, imaginary = sums[chunk % 2, :128, lanes], sums[chunk % 2, 128:, lanes]
             cosine, sine = twist[0, lanes, :], twist[1, lanes, :]
             turned[span, part * 128 : (part + 1) * 128] = (real * cosine - imaginary * sine).astype(jnp.bfloat16)
             turned[span, 512 + part * 128 : 640 + part * 128] = (imaginary * cosine + real * sine).astype(
                 jnp.bfloat16
             )
     low = lax.broadcasted_iota(jnp.int32, (128, 128), 1) < HALF
+    follow[0].wait()
     sent = []
     for chunk in range(4):
-        follow[chunk].wait()
-        sums[...] = lax.dot_general(
+        sums[chunk % 2] = lax.dot_general(
             last[chunk * 256 : (chunk + 1) * 256, :],
             turned[...],
             (((1,), (1,)), ((), ())),
             preferred_element_type=jnp.float32,
         )
         for pair in range(4):
-            even = sums[:128, pair * 128 : (pair + 1) * 128]
-            odd = sums[128:, pair * 128 : (pair + 1) * 128]
+            even = sums[chunk % 2, :128, pair * 128 : (pair + 1) * 128]
+            odd = sums[chunk % 2, 128:, pair * 128 : (pair + 1) * 128]
             stage[chunk % 2, pl.ds(2 * pair, 128, stride=8), :] = jnp.where(low, even, pltpu.roll(odd, HALF, 1))
             stage[chunk % 2, pl.ds(2 * pair + 1, 128, stride=8), :] = jnp.where(low, pltpu.roll(even, HALF, 1), odd)
         plane, base = chunk // 2, (chunk % 2) * 128
@@ -366,9 +366,9 @@
             out[plane, :, (base + group) * 128 : (base + group + 1) * 128] = stage[
                 chunk % 2, group * 8 : (group + 1) * 8, :
             ].astype(jnp.bfloat16)
-        lanes = pl.ds(base * 128, A // 2)
-        sent.append(pltpu.make_async_copy(out.at[plane, :, lanes], out_ref.at[plane, :, lanes], went.at[chunk]))
-        sent[-1].start()
+        if chunk % 2 == 1:
+            sent.append(pltpu.make_async_copy(out.at[plane], out_ref.at[plane], went.at[plane]))
+            sent[-1].start()
     for copy in sent:
         copy.wait()
 
@@ -385,11 +385,11 @@
             pltpu.VMEM((2, 512, 128), jnp.float32),
             pltpu.VMEM((1024, 512), jnp.bfloat16),
             pltpu.VMEM((512, 1024), jnp.bfloat16),
-            pltpu.VMEM((256, 512), jnp.float32),
+            pltpu.VMEM((2, 256, 512), jnp.float32),
             pltpu.VMEM((2, 1024, 128), jnp.float32),
             pltpu.VMEM((2, ROWS, A), jnp.bfloat16),
-            pltpu.SemaphoreType.DMA((3, 4)),
-            pltpu.SemaphoreType.DMA((4,)),
+            pltpu.SemaphoreType.DMA((3, 1)),
+            pltpu.SemaphoreType.DMA((2,)),
         ],
         compiler_params=pltpu.CompilerParams(vmem_limit_bytes=50 * MIB),
         name="inverse",

time: 135 us -> 133 us (0.985)
  transfers between devices with their start and end apart: 2 -> 2, of which waited for: 2 -> 2; matrix products, arithmetic and copies ran while one was open for 3% -> 4% of each run, Pallas kernels for 2% -> 2%
where the time goes in v4:
time: 133 us
  waiting for transfers between devices  57.5 us (43%)
  blocking collectives  41.3 us (31%)
  Pallas kernels  15.1 us (11%)
  starting transfers between devices  14.1 us (11%)
  local copies, waits for them, and re-layouts  2.75 us (2%)
  other arithmetic  1.95 us (1%)
    all_to_all x1, blocking collectives, body(): piece = lax.all_to_all(pack(echoes), 'az', 0, 0, tiled=True)  41.3 us
    all_to_all x1, waiting for transfers between devices, body(): moved = lax.all_to_all(moved, ('rg', 'az'), 0, 0, tiled=True)  29.5 us
    all_to_all x1, waiting for transfers between devices, body(): lax.all_to_all(spectrum.reshape(256, 16, 128), ('rg', 'az'), 0, 0, tiled=...  28 us
    all_to_all x1, starting transfers between devices, body(): lax.all_to_all(spectrum.reshape(256, 16, 128), ('rg', 'az'), 0, 0, tiled=...  8.87 us
    pallas_call x1, Pallas kernels, inverse(): pl.pallas_call(inverse_kernel, out_shape=jax.ShapeDtypeStruct((2, ROWS, A...  5.43 us
    all_to_all x1, starting transfers between devices, body(): moved = lax.all_to_all(moved, ('rg', 'az'), 0, 0, tiled=True)  5.19 us
    pallas_call x1, Pallas kernels, forward(): pl.pallas_call(forward_kernel, out_shape=jax.ShapeDtypeStruct((64, 4, 16,...  3.71 us
  transfers between devices with their start and end apart: 2, of which 2 were waited for; matrix products, arithmetic and copies ran while one was open for 4% of the time, Pallas kernels for 2%

profile of v4, /device:TPU:1, one launch (start us, length us, event | category | flops | bytes accessed | tf_op | source)
XLA Modules:
  0.0 132.8 jit_solution(13967248876889101798)
XLA Ops:
  0.0 2.2 %pack.1 = bf16[64,16,512]{2,1,0:T(8,128)(2,1)S(1)} custom-call(bf16[2,512,512]{2,1,0:T(8,128)(2,1)} %echo_ref.1), custom_call_target="tpu_custom_call" | custom-call | tf_op jit(solution)/shard_map/pack/pallas_call | solution.py:103
  2.2 41.3 %all_to_all.15 = bf16[64,16,512]{2,1,0:T(8,128)(2,1)S(1)} all-to-all(bf16[64,16,512]{2,1,0:T(8,128)(2,1)S(1)} %pack.1), channel_id=1, replica_groups=mesh['az'=64,'rg'=4] {'az'}, dimensions={0} | all-to-all | bytes 2097152 | tf_op jit(solution)/shard_map/all_to_all | solution.py:405
  43.5 0.0 copy-done
  43.5 0.0 copy-done.2
  43.5 3.7 %forward.1 = bf16[64,4,16,128]{3,2,1,0:T(8,128)(2,1)} custom-call(bf16[1024,512]{1,0:T(8,128)(2,1)S(1)} %bitcast.4, bf16[1024,1024]{1,0:T(8,128)(2,1)S(1)} %copy-done, f32[2,512,128]{2,1,0:T(8,128)S(1)} %copy-done.2, bf16[1024,1024]{1,0:T(8,128)(2,1)} %constant.33.clone.second_ref), custom_call_target="tpu_custom_call" | custom-call | tf_op jit(solution)/shard_map/forward/pallas_call | solution.py:168
  47.2 0.0 copy-start.3
  47.3 0.0 copy-start.4
  47.3 0.0 copy-start.5
  47.3 0.0 copy-start.1
  47.3 8.9 %all-to-all-start.1 = ((bf16[256,16,128]{2,1,0:T(8,128)(2,1)}), bf16[256,16,128]{2,1,0:T(8,128)(2,1)S(1)}, u32[]{:S(2)}, u32[]{:S(2)}) async-start(bf16[256,16,128]{2,1,0:T(8,128)(2,1)} %bitcast.1), calls=%async_computation.1 | async-start | bytes 2097152 | tf_op jit(solution)/shard_map/all_to_all | solution.py:407
  56.2 0.0 copy-done.3
  56.2 0.6 dynamic_slice.14
  56.8 0.6 dynamic_slice.13
  57.4 0.6 dynamic_slice.12
  58.1 2.0 %pad_add_fusion.band_ref = s32[3]{0:T(128)S(1)} fusion(s32[1]{0:T(128)} %dynamic_slice.14, s32[1]{0:T(128)} %dynamic_slice.13, s32[1]{0:T(128)} %dynamic_slice.12), kind=kLoop, calls=%fused_computation | loop fusion | flops 6 | bytes 24 | tf_op jit(solution)/shard_map/stack | solution.py:403
  60.0 0.6 taps.1
  60.6 28.0 %all-to-all-done.1.spectrum_ref = bf16[256,16,128]{2,1,0:T(8,128)(2,1)S(1)} async-done(((bf16[256,16,128]{2,1,0:T(8,128)(2,1)}), bf16[256,16,128]{2,1,0:T(8,128)(2,1)S(1)}, u32[]{:S(2)}, u32[]{:S(2)}) %all-to-all-start.1) | async-done | bytes 1048608 | tf_op jit(solution)/shard_map/all_to_all | solution.py:407
  88.6 1.8 %migrate.1 = bf16[256,16,128]{2,1,0:T(8,128)(2,1)} custom-call(bf16[256,16,128]{2,1,0:T(8,128)(2,1)S(1)} %all-to-all-done.1.spectrum_ref, bf16[256,768]{1,0:T(8,128)(2,1)S(1)} %taps.1), custom_call_target="tpu_custom_call" | custom-call | tf_op jit(solution)/shard_map/migrate/pallas_call | solution.py:245
  90.4 5.2 %all-to-all-start.2 = ((bf16[256,16,128]{2,1,0:T(8,128)(2,1)}), bf16[256,16,128]{2,1,0:T(8,128)(2,1)S(1)}, u32[]{:S(2)}, u32[]{:S(2)}) async-start(bf16[256,16,128]{2,1,0:T(8,128)(2,1)} %migrate.1), calls=%async_computation.2 | async-start | bytes 2097152 | tf_op jit(solution)/shard_map/all_to_all | solution.py:409
  95.6 0.8 dynamic_slice.15
  96.3 0.1 broadcast_in_dim.2.rate_ref
  96.4 1.5 %phases.1.phase_ref = f32[2,64,4,8,128]{4,3,2,1,0:T(8,128)S(1)} custom-call(f32[8,128]{1,0:T(8,128)S(1)} %broadcast_in_dim.2.rate_ref), custom_call_target="tpu_custom_call" | custom-call | flops 20000000 | bytes 2100000 | tf_op jit(solution)/shard_map/phases/pallas_call | solution.py:290
  97.9 29.5 %all-to-all-done.2 = bf16[256,16,128]{2,1,0:T(8,128)(2,1)S(1)} async-done(((bf16[256,16,128]{2,1,0:T(8,128)(2,1)}), bf16[256,16,128]{2,1,0:T(8,128)(2,1)S(1)}, u32[]{:S(2)}, u32[]{:S(2)}) %all-to-all-start.2) | async-done | bytes 1048608 | tf_op jit(solution)/shard_map/all_to_all | solution.py:409
  127.4 5.4 %inverse.1 = bf16[2,8,32768]{2,1,0:T(8,128)(2,1)} custom-call(bf16[64,4,16,128]{3,2,1,0:T(8,128)(2,1)S(1)} %bitcast.3, f32[2,64,4,8,128]{4,3,2,1,0:T(8,128)S(1)} %phases.1.phase_ref, bf16[1024,1024]{1,0:T(8,128)(2,1)} %constant.34.clone.third_ref, bf16[1024,1024]{1,0:T(8,128)(2,1)} %constant.35.clone.last_ref, f32[8,512,128]{2,1,0:T(8,128)} %constant.36.clone.twist_ref), custom_call_target="tpu_custom_call" | custom-call | tf_op jit(solution)/shard_map/inverse/pallas_call | solution.py:377
  (5 shorter events, 0.0 us)
Async XLA Ops:
  0.0 43.5 %copy-start = (bf16[1024,1024]{1,0:T(8,128)(2,1)S(1)}, bf16[1024,1024]{1,0:T(8,128)(2,1)}, u32[]{:S(2)}) copy-start(bf16[1024,1024]{1,0:T(8,128)(2,1)} %constant.31.clone.first) | copy-start | bytes 6291460
  0.0 43.5 %copy-start.2 = (f32[2,512,128]{2,1,0:T(8,128)S(1)}, f32[2,512,128]{2,1,0:T(8,128)}, u32[]{:S(2)}) copy-start(f32[2,512,128]{2,1,0:T(8,128)} %constant.32.clone.twist) | copy-start | bytes 1572868
  47.2 8.9 %copy-start.3 = (s32[256]{0:T(256)S(1)}, s32[256]{0:T(256)}, u32[]{:S(2)}) copy-start(s32[256]{0:T(256)} %param.16) | copy-start | bytes 3076
  47.3 9.6 %copy-start.4 = (s32[256]{0:T(256)S(1)}, s32[256]{0:T(256)}, u32[]{:S(2)}) copy-start(s32[256]{0:T(256)} %param.15) | copy-start | bytes 3076
  47.3 10.2 %copy-start.5 = (s32[256]{0:T(256)S(1)}, s32[256]{0:T(256)}, u32[]{:S(2)}) copy-start(s32[256]{0:T(256)} %param.14) | copy-start | bytes 3076
  47.3 12.8 %copy-start.1 = (bf16[8,5,128,128]{3,2,1,0:T(8,128)(2,1)S(1)}, bf16[8,5,128,128]{3,2,1,0:T(8,128)(2,1)}, u32[]{:S(2)}) copy-start(bf16[8,5,128,128]{3,2,1,0:T(8,128)(2,1)} %coef_ref.1) | copy-start | bytes 3932164
  47.3 41.3 %all-to-all-start.1 = ((bf16[256,16,128]{2,1,0:T(8,128)(2,1)}), bf16[256,16,128]{2,1,0:T(8,128)(2,1)S(1)}, u32[]{:S(2)}, u32[]{:S(2)}) async-start(bf16[256,16,128]{2,1,0:T(8,128)(2,1)} %bitcast.1), calls=%async_computation.1 | async-start | bytes 2097152 | tf_op jit(solution)/shard_map/all_to_all | solution.py:407
  90.4 37.0 %all-to-all-start.2 = ((bf16[256,16,128]{2,1,0:T(8,128)(2,1)}), bf16[256,16,128]{2,1,0:T(8,128)(2,1)S(1)}, u32[]{:S(2)}, u32[]{:S(2)}) async-start(bf16[256,16,128]{2,1,0:T(8,128)(2,1)} %migrate.1), calls=%async_computation.2 | async-start | bytes 2097152 | tf_op jit(solution)/shard_map/all_to_all | solution.py:409

commit v5 on v4

--- a/solution.py
+++ b/solution.py
@@ -20,7 +20,7 @@
 HT = 2
 WMAX = 5
 ROWS = 8
-PACKS = 8
+PACKS = 2
 HALF = 64
 MIB = 1024 * 1024
 FAR = pltpu.MemorySpace.HBM
@@ -319,7 +319,7 @@
     lead = fetch(third_ref, third, came.at[0], 1)
     turns = fetch(twist_ref.at[:2], twist, came.at[1], 1)
     follow = fetch(last_ref, last, came.at[2], 1)
-    for copy in lead + turns + follow:
+    for copy in lead + turns:
         copy.start()
     for chunk in range(4):
         for part in range(4):
@@ -333,6 +333,7 @@
             focused[chunk * 256 : (chunk + 1) * 256, part * FB : (part + 1) * FB] = both.reshape(256, FB)
     lead[0].wait()
     turns[0].wait()
+    follow[0].start()
     for chunk in range(4):
         sums[chunk % 2] = jnp.dot(
             third[chunk * 256 : (chunk + 1) * 256, :], focused[...], preferred_element_type=jnp.float32

time: 133 us -> 133 us (level)
  no operation moved by 1% of the time
where the time goes in v5:
time: 133 us
  waiting for transfers between devices  57.5 us (43%)
  blocking collectives  41.3 us (31%)
  Pallas kernels  15 us (11%)
  starting transfers between devices  14.1 us (11%)
  local copies, waits for them, and re-layouts  2.75 us (2%)
  other arithmetic  1.95 us (1%)
    all_to_all x1, blocking collectives, body(): piece = lax.all_to_all(pack(echoes), 'az', 0, 0, tiled=True)  41.3 us
    all_to_all x1, waiting for transfers between devices, body(): moved = lax.all_to_all(moved, ('rg', 'az'), 0, 0, tiled=True)  29.5 us
    all_to_all x1, waiting for transfers between devices, body(): lax.all_to_all(spectrum.reshape(256, 16, 128), ('rg', 'az'), 0, 0, tiled=...  28 us
    all_to_all x1, starting transfers between devices, body(): lax.all_to_all(spectrum.reshape(256, 16, 128), ('rg', 'az'), 0, 0, tiled=...  8.87 us
    pallas_call x1, Pallas kernels, inverse(): pl.pallas_call(inverse_kernel, out_shape=jax.ShapeDtypeStruct((2, ROWS, A...  5.59 us
    all_to_all x1, starting transfers between devices, body(): moved = lax.all_to_all(moved, ('rg', 'az'), 0, 0, tiled=True)  5.19 us
    pallas_call x1, Pallas kernels, forward(): pl.pallas_call(forward_kernel, out_shape=jax.ShapeDtypeStruct((64, 4, 16,...  3.71 us
  transfers between devices with their start and end apart: 2, of which 2 were waited for; matrix products, arithmetic and copies ran while one was open for 4% of the time, Pallas kernels for 2%

profile of v5, /device:TPU:1, one launch (start us, length us, event | category | flops | bytes accessed | tf_op | source)
XLA Modules:
  0.0 132.7 jit_solution(15275881383606552996)
XLA Ops:
  0.0 1.9 %pack.1 = bf16[64,16,512]{2,1,0:T(8,128)(2,1)S(1)} custom-call(bf16[2,512,512]{2,1,0:T(8,128)(2,1)} %echo_ref.1), custom_call_target="tpu_custom_call" | custom-call | tf_op jit(solution)/shard_map/pack/pallas_call | solution.py:103
  1.9 41.3 %all_to_all.15 = bf16[64,16,512]{2,1,0:T(8,128)(2,1)S(1)} all-to-all(bf16[64,16,512]{2,1,0:T(8,128)(2,1)S(1)} %pack.1), channel_id=1, replica_groups=mesh['az'=64,'rg'=4] {'az'}, dimensions={0} | all-to-all | bytes 2097152 | tf_op jit(solution)/shard_map/all_to_all | solution.py:406
  43.3 0.0 copy-done
  43.3 0.0 copy-done.2
  43.3 3.7 %forward.1 = bf16[64,4,16,128]{3,2,1,0:T(8,128)(2,1)} custom-call(bf16[1024,512]{1,0:T(8,128)(2,1)S(1)} %bitcast.4, bf16[1024,1024]{1,0:T(8,128)(2,1)S(1)} %copy-done, f32[2,512,128]{2,1,0:T(8,128)S(1)} %copy-done.2, bf16[1024,1024]{1,0:T(8,128)(2,1)} %constant.33.clone.second_ref), custom_call_target="tpu_custom_call" | custom-call | tf_op jit(solution)/shard_map/forward/pallas_call | solution.py:168
  47.0 0.0 copy-start.3
  47.0 0.0 copy-start.4
  47.0 0.0 copy-start.5
  47.0 0.0 copy-start.1
  47.0 8.9 %all-to-all-start.1 = ((bf16[256,16,128]{2,1,0:T(8,128)(2,1)}), bf16[256,16,128]{2,1,0:T(8,128)(2,1)S(1)}, u32[]{:S(2)}, u32[]{:S(2)}) async-start(bf16[256,16,128]{2,1,0:T(8,128)(2,1)} %bitcast.1), calls=%async_computation.1 | async-start | bytes 2097152 | tf_op jit(solution)/shard_map/all_to_all | solution.py:408
  55.9 0.6 dynamic_slice.14
  56.6 0.6 dynamic_slice.13
  57.2 0.0 copy-done.5
  57.2 0.6 dynamic_slice.12
  57.8 2.0 %pad_add_fusion.band_ref = s32[3]{0:T(128)S(1)} fusion(s32[1]{0:T(128)} %dynamic_slice.14, s32[1]{0:T(128)} %dynamic_slice.13, s32[1]{0:T(128)} %dynamic_slice.12), kind=kLoop, calls=%fused_computation | loop fusion | flops 6 | bytes 24 | tf_op jit(solution)/shard_map/stack | solution.py:404
  59.8 0.6 taps.1
  60.4 28.0 %all-to-all-done.1.spectrum_ref = bf16[256,16,128]{2,1,0:T(8,128)(2,1)S(1)} async-done(((bf16[256,16,128]{2,1,0:T(8,128)(2,1)}), bf16[256,16,128]{2,1,0:T(8,128)(2,1)S(1)}, u32[]{:S(2)}, u32[]{:S(2)}) %all-to-all-start.1) | async-done | bytes 1048608 | tf_op jit(solution)/shard_map/all_to_all | solution.py:408
  88.4 1.8 %migrate.1 = bf16[256,16,128]{2,1,0:T(8,128)(2,1)} custom-call(bf16[256,16,128]{2,1,0:T(8,128)(2,1)S(1)} %all-to-all-done.1.spectrum_ref, bf16[256,768]{1,0:T(8,128)(2,1)S(1)} %taps.1), custom_call_target="tpu_custom_call" | custom-call | tf_op jit(solution)/shard_map/migrate/pallas_call | solution.py:245
  90.1 5.2 %all-to-all-start.2 = ((bf16[256,16,128]{2,1,0:T(8,128)(2,1)}), bf16[256,16,128]{2,1,0:T(8,128)(2,1)S(1)}, u32[]{:S(2)}, u32[]{:S(2)}) async-start(bf16[256,16,128]{2,1,0:T(8,128)(2,1)} %migrate.1), calls=%async_computation.2 | async-start | bytes 2097152 | tf_op jit(solution)/shard_map/all_to_all | solution.py:410
  95.3 0.8 dynamic_slice.15
  96.1 0.1 broadcast_in_dim.2.rate_ref
  96.2 1.5 %phases.1.phase_ref = f32[2,64,4,8,128]{4,3,2,1,0:T(8,128)S(1)} custom-call(f32[8,128]{1,0:T(8,128)S(1)} %broadcast_in_dim.2.rate_ref), custom_call_target="tpu_custom_call" | custom-call | flops 20000000 | bytes 2100000 | tf_op jit(solution)/shard_map/phases/pallas_call | solution.py:290
  97.6 29.5 %all-to-all-done.2 = bf16[256,16,128]{2,1,0:T(8,128)(2,1)S(1)} async-done(((bf16[256,16,128]{2,1,0:T(8,128)(2,1)}), bf16[256,16,128]{2,1,0:T(8,128)(2,1)S(1)}, u32[]{:S(2)}, u32[]{:S(2)}) %all-to-all-start.2) | async-done | bytes 1048608 | tf_op jit(solution)/shard_map/all_to_all | solution.py:410
  127.1 5.6 %inverse.1 = bf16[2,8,32768]{2,1,0:T(8,128)(2,1)} custom-call(bf16[64,4,16,128]{3,2,1,0:T(8,128)(2,1)S(1)} %bitcast.3, f32[2,64,4,8,128]{4,3,2,1,0:T(8,128)S(1)} %phases.1.phase_ref, bf16[1024,1024]{1,0:T(8,128)(2,1)} %constant.34.clone.third_ref, bf16[1024,1024]{1,0:T(8,128)(2,1)} %constant.35.clone.last_ref, f32[8,512,128]{2,1,0:T(8,128)} %constant.36.clone.twist_ref), custom_call_target="tpu_custom_call" | custom-call | tf_op jit(solution)/shard_map/inverse/pallas_call | solution.py:378
  (5 shorter events, 0.0 us)
Async XLA Ops:
  0.0 43.3 %copy-start = (bf16[1024,1024]{1,0:T(8,128)(2,1)S(1)}, bf16[1024,1024]{1,0:T(8,128)(2,1)}, u32[]{:S(2)}) copy-start(bf16[1024,1024]{1,0:T(8,128)(2,1)} %constant.31.clone.first) | copy-start | bytes 6291460
  0.0 43.3 %copy-start.2 = (f32[2,512,128]{2,1,0:T(8,128)S(1)}, f32[2,512,128]{2,1,0:T(8,128)}, u32[]{:S(2)}) copy-start(f32[2,512,128]{2,1,0:T(8,128)} %constant.32.clone.twist) | copy-start | bytes 1572868
  47.0 8.9 %copy-start.3 = (s32[256]{0:T(256)S(1)}, s32[256]{0:T(256)}, u32[]{:S(2)}) copy-start(s32[256]{0:T(256)} %param.16) | copy-start | bytes 3076
  47.0 9.6 %copy-start.4 = (s32[256]{0:T(256)S(1)}, s32[256]{0:T(256)}, u32[]{:S(2)}) copy-start(s32[256]{0:T(256)} %param.15) | copy-start | bytes 3076
  47.0 10.2 %copy-start.5 = (s32[256]{0:T(256)S(1)}, s32[256]{0:T(256)}, u32[]{:S(2)}) copy-start(s32[256]{0:T(256)} %param.14) | copy-start | bytes 3076
  47.0 12.8 %copy-start.1 = (bf16[8,5,128,128]{3,2,1,0:T(8,128)(2,1)S(1)}, bf16[8,5,128,128]{3,2,1,0:T(8,128)(2,1)}, u32[]{:S(2)}) copy-start(bf16[8,5,128,128]{3,2,1,0:T(8,128)(2,1)} %coef_ref.1) | copy-start | bytes 3932164
  47.0 41.3 %all-to-all-start.1 = ((bf16[256,16,128]{2,1,0:T(8,128)(2,1)}), bf16[256,16,128]{2,1,0:T(8,128)(2,1)S(1)}, u32[]{:S(2)}, u32[]{:S(2)}) async-start(bf16[256,16,128]{2,1,0:T(8,128)(2,1)} %bitcast.1), calls=%async_computation.1 | async-start | bytes 2097152 | tf_op jit(solution)/shard_map/all_to_all | solution.py:408
  90.1 37.0 %all-to-all-start.2 = ((bf16[256,16,128]{2,1,0:T(8,128)(2,1)}), bf16[256,16,128]{2,1,0:T(8,128)(2,1)S(1)}, u32[]{:S(2)}, u32[]{:S(2)}) async-start(bf16[256,16,128]{2,1,0:T(8,128)(2,1)} %migrate.1), calls=%async_computation.2 | async-start | bytes 2097152 | tf_op jit(solution)/shard_map/all_to_all | solution.py:410
